TPU v7x, 128 devices: a whole 4x4x4 slice. The times are simulated.
128 devices in a mesh: ta: 8 (over y_lo, x), gz: 8 (over z, core), col: 2 (over y_hi).
Axes of the slice: x: 4, y: 4 (y_hi: 2, y_lo: 2; y = y_hi * 2 + y_lo), z: 4, core: 2. Of those that a mesh axis runs over, the one named last changes fastest.
Arguments:
- rhs_field: float32 [1, 96, 64, 32, 128], P(None, None, ('ta', 'col'), 'gz'), may hold values from -6 to 6
- link_weights: float32 [8, 64, 32, 128], P(None, ('ta', 'col'), 'gz'), may hold values from 0.4 to 1.6
- fine_blocks: float32 [9, 96, 96], replicated, may hold values from -1 to 5
- smoother: float32 [96, 96], replicated, may hold values from -1 to 1
- plane_next: int32 [4, 128], replicated, may hold values from 0 to 127, as said below
- aggregate: int32 [128], replicated, may hold values from 0 to 7, as said below
- restrict_map: float32 [96, 128], replicated, may hold values from -0.625 to 0.625
- prolong_map: float32 [128, 96], replicated, may hold values from -0.5 to 0.5
- coarse_blocks: float32 [9, 128, 128], replicated, may hold values from -1 to 5
- coarse_smoother: float32 [128, 128], replicated, may hold values from -1 to 1
- coarse_next: int32 [4, 8], replicated, may hold values from 0 to 7, as said below
Outputs:
- solution: float32 [1, 96, 64, 32, 128], P(None, None, ('ta', 'col'), 'gz')
- residual: float32 [1, 96, 64, 32, 128], P(None, None, ('ta', 'col'), 'gz')
Inputs may be any that keep to these rules, and one draw needn't show every extreme that they name: `plane_next`: each row is an ordering of the plane sites; row 1 undoes row 0 and row 3 undoes row 2. `aggregate`: each coarse plane site is named by exactly 16 entries. `coarse_next`: each row is an ordering of the coarse plane sites; row 1 undoes row 0 and row 3 undoes row 2.
All inputs are finite; a program needn't handle non-finite values.
Results may differ from a plain program's by a relative error of at most 0.0003.
Values sent between devices are 32-bit elements; how exact they have to be, the bound alone decides.
No kernel may reach another device: no remote copies, remote signals or barrier semaphores. Data moves between devices by JAX's collectives and lax.ppermute only.
A program may use at most 64 MiB of HBM per device.

v0:
```python
import jax
import jax.numpy as jnp
from jax import lax
from jax.experimental import pallas as pl
from jax.experimental.pallas import tpu as pltpu
from jax.sharding import PartitionSpec as P


F32, BF16 = jnp.float32, jnp.bfloat16
CF, CC, PL, NB, CP = 96, 128, 128, 9, 8
KF, KC = NB * CF, NB * CC
SWEEPS = 3
TAXES = ("ta", "col")


def halves(value):
    high = value.astype(BF16)
    return high, (value - high.astype(F32)).astype(BF16)


def dot(left, right):
    return jnp.dot(left, right, preferred_element_type=F32)


def dot_nt(left, right):
    return lax.dot_general(left, right, (((1,), (1,)), ((), ())), preferred_element_type=F32)


def lanes_of(value, index):
    return jnp.take_along_axis(value, index, axis=1)


def product(matrix, high, low):
    both = dot(matrix[...], high[...])
    return both[0:CF] + both[CF : 2 * CF] + dot(matrix[0:CF, :], low[...])


def put(high, low, row, column, value):
    top, rest = halves(value)
    rows, columns = pl.ds(row, CF), pl.ds(column * PL, PL)
    high[rows, columns] = top
    low[rows, columns] = rest


def fill(field, site, stride, weights, plane, high, low, column):
    here = field[site]
    put(high, low, 0, column, here)
    for hop, offset in enumerate((stride, -stride, 1, -1)):
        put(high, low, (hop + 1) * CF, column, field[site + offset] * weights[hop : hop + 1])
    for hop in range(4):
        there = lanes_of(here, plane[hop]) * weights[hop + 4 : hop + 5]
        put(high, low, (hop + 5) * CF, column, there)


def place(t, z):
    return (t + 2) * 8 + z + 2


def middle_pair(index):
    return 1 + lax.div(index, 3), 2 * lax.rem(index, 3) - 1


def edge_pair(index):
    return 3 * lax.div(index, 3), 2 * lax.rem(index, 3) - 1


def outer_pair(index):
    return 5 * lax.div(index, 2) - 1, 2 * lax.rem(index, 2)


def each(count, load, finish):
    load(0, 0)

    def body(index, carry):
        load(2 * index + 1, 1)
        finish(2 * index, 0)
        load(2 * index + 2, 0)
        finish(2 * index + 1, 1)
        return carry

    lax.fori_loop(0, count // 2 - 1, body, 0)
    load(count - 1, 1)
    finish(count - 2, 0)
    finish(count - 1, 1)


def plane_tables(ref):
    return [jnp.broadcast_to(ref[hop : hop + 1, :], (CF, PL)) for hop in range(4)]


def smooth(smat, high, low, x0, sources, targets):
    for column, source in enumerate(sources):
        put(high, low, 0, column, source)
    value = product(smat, high.at[0:CF], low.at[0:CF])
    for column, target in enumerate(targets):
        x0[target] = value[:, column * PL : (column + 1) * PL]


def sweeps(count, where, matrix, field, x0, lw, plane, vhigh, vlow, target):
    def load(index, slot):
        site = place(*where(index))
        for column in range(2):
            fill(field, site + column, 8, lw[site + column], plane, vhigh.at[slot], vlow.at[slot], column)

    def finish(index, slot):
        site = place(*where(index))
        change = product(matrix, vhigh.at[slot], vlow.at[slot])
        for column in range(2):
            old = field[site + column] + x0[site + column]
            target[site + column] = old - change[:, column * PL : (column + 1) * PL]

    each(count, load, finish)


def block_pairs(rows, matrix, field, lw, plane, vhigh, vlow, finish):
    pairs = [(t, half) for t in rows for half in range(2)]

    def load(t, half):
        site = place(t, 2 * half)
        for column in range(2):
            fill(field, site + column, 8, lw[site + column], plane, vhigh.at[half], vlow.at[half], column)

    load(*pairs[0])
    for number, (t, half) in enumerate(pairs):
        if number + 1 < len(pairs):
            load(*pairs[number + 1])
        image = product(matrix, vhigh.at[half], vlow.at[half])
        finish(t, half, [image[:, 0:PL], image[:, PL : 2 * PL]])


def blank_rows(field, first, count):
    for t in (-1, 4):
        field[pl.ds(place(t, first), count)] = jnp.zeros((count, CF, PL), F32)


def one_hop(matrix, values, vhigh, vlow, slot):
    for column, value in enumerate(values):
        put(vhigh.at[slot], vlow.at[slot], 0, column, value)
    image = product(matrix, vhigh.at[slot, 0:CF], vlow.at[slot, 0:CF])
    return [image[:, 0:PL], image[:, PL : 2 * PL]]


def close_edges(hops, field, lw, vhigh, vlow, target):
    for number, (t, outside, hop) in enumerate(((3, 4, 0), (0, -1, 1))):
        for pair in range(3):
            z = 2 * pair - 1
            here, there = place(t, z), place(outside, z)
            values = [field[there + c] * lw[here + c, hop : hop + 1, :] for c in range(2)]
            changes = one_hop(hops.at[hop], values, vhigh, vlow, (number + pair) % 2)
            for c in range(2):
                target[here + c] = target[here + c] - changes[c]


def exact_dot(left, right):
    parts = []
    for value in (left, right):
        top, rest = halves(value)
        tail = (value - top.astype(F32) - rest.astype(F32)).astype(BF16)
        parts.append((top, rest, tail))
    (l0, l1, l2), (r0, r1, r2) = parts
    small = dot(l0, r2) + dot(l1, r1) + dot(l2, r0)
    return small + (dot(l0, r1) + dot(l1, r0)) + dot(l0, r0)


def pair_matrix(target, row, depth, value):
    high, low = halves(value)
    target[row : row + CC, 0:CC] = high
    target[row : row + CC, CC : 2 * CC] = low
    target[depth + row : depth + row + CC, 0:CC] = high
    target[depth + row : depth + row + CC, CC : 2 * CC] = jnp.zeros((CC, CC), BF16)


def prepare_kernel(s_ref, blocks, cs_ref, coarse, smat, mmat, bmat, cmat, csmat, mhops, bhops):
    smooth_matrix = s_ref[...]
    smat[0:CF, :], smat[CF : 2 * CF, :] = halves(smooth_matrix)
    whole = jnp.concatenate([blocks[k] for k in range(NB)], axis=1)
    bmat[0:CF, :], bmat[CF : 2 * CF, :] = halves(whole)
    mmat[0:CF, :], mmat[CF : 2 * CF, :] = halves(exact_dot(smooth_matrix, whole))
    for hop in range(2):
        block = blocks[hop + 1]
        bhops[hop, 0:CF, :], bhops[hop, CF : 2 * CF, :] = halves(block)
        mhops[hop, 0:CF, :], mhops[hop, CF : 2 * CF, :] = halves(exact_dot(smooth_matrix, block))
    coarse_smooth = cs_ref[...]
    for k in range(NB):
        pair_matrix(cmat, k * CC, KC, jnp.transpose(exact_dot(coarse_smooth, coarse[k]), (1, 0)))
    pair_matrix(csmat, 0, CC, jnp.transpose(coarse_smooth, (1, 0)))


def local_kernel(
    a0, a1, a2, a3, l_ref, hzm, hzp, smat, mmat, plane_ref,
    x0, lw, x1,
    vhigh, vlow,
):
    plane = plane_tables(plane_ref)
    for t, row in enumerate((a0, a1, a2, a3)):
        for pair in range(2):
            site = place(t, 2 * pair)
            slot = pair
            smooth(smat, vhigh.at[slot], vlow.at[slot], x0, [row[2 * pair], row[2 * pair + 1]], [site, site + 1])
        for z in range(4):
            lw[place(t, z)] = l_ref[:, 4 * t + z, :]
        for slot, (source, z) in enumerate(((hzm, -2), (hzp, 4))):
            site = place(t, z)
            smooth(
                smat, vhigh.at[slot], vlow.at[slot], x0,
                [source[2 * t, 0:CF, :], source[2 * t + 1, 0:CF, :]], [site, site + 1],
            )
        lw[place(t, -1)] = hzm[2 * t + 1, CF : CF + 8, :]
        lw[place(t, 4)] = hzp[2 * t, CF : CF + 8, :]

    blank_rows(x0, -1, 6)
    blank_rows(x1, 0, 4)
    sweeps(6, middle_pair, mmat, x0, x0, lw, plane, vhigh, vlow, x1)


def edge_kernel(x0, lw, x1_in, mmat, plane_ref, x1, vhigh, vlow):
    plane = plane_tables(plane_ref)
    sweeps(6, edge_pair, mmat, x0, x0, lw, plane, vhigh, vlow, x1)


def pre_kernel(
    a0, a1, a2, a3, tm1, tp1, ctm, ctp, smat, bmat, mhops, bhops, r_ref, plane_ref, member_ref,
    x0_in, lw_in, x1_in,
    x0, lw, x1, up_out, down_out, first_out, last_out,
    vhigh, vlow, summed,
):
    plane = plane_tables(plane_ref)
    for source, t in ((tm1, -1), (tp1, 4)):
        for slot in range(2):
            site = place(t, 2 * slot)
            smooth(
                smat, vhigh.at[slot], vlow.at[slot], x0,
                [source[2 * slot, 0:CF, :], source[2 * slot + 1, 0:CF, :]], [site, site + 1],
            )
        lw[pl.ds(place(t, 0), 4)] = source[:, CF : CF + 8, :]
    for slot, (source, t) in enumerate(((ctm, -1), (ctp, 4))):
        smooth(
            smat, vhigh.at[slot], vlow.at[slot], x0,
            [source[0], source[1]], [place(t, -1), place(t, 4)],
        )

    close_edges(mhops, x0, lw, vhigh, vlow, x1)
    first_out[...] = x1[pl.ds(place(0, 0), 4)]
    last_out[...] = x1[pl.ds(place(3, 0), 4)]

    member = member_ref[...].astype(BF16)
    rows = (a0, a1, a2, a3)

    def restrict(number, value):
        top, tail = halves(value)
        total = dot_nt(member, top) + dot_nt(member, tail)
        summed[number * 8 : number * 8 + 8, :] = total[0:8]

    def finish(t, half, images):
        for column, image in enumerate(images):
            restrict(4 * t + 2 * half + column, rows[t][2 * half + column] - image)

    block_pairs(range(4), bmat, x1, lw, plane, vhigh, vlow, finish)
    for base, t, outside, hop in ((16, 3, 4, 1), (20, 0, -1, 0)):
        for half in range(2):
            here, there = place(t, 2 * half), place(outside, 2 * half)
            values = [x1[here + c] * lw[there + c, hop : hop + 1, :] for c in range(2)]
            images = one_hop(bhops.at[hop], values, vhigh, vlow, half)
            for c in range(2):
                restrict(base + 2 * half + c, -images[c])
    top, tail = halves(summed[...])
    rtop, rtail = halves(r_ref[...])
    crhs = dot(top, rtop) + dot(tail, rtop) + dot(top, rtail)
    crhs = crhs.reshape(24, CP, CC)
    up_out[...] = crhs[0:20]
    down_out[0:16] = crhs[0:16]
    down_out[16:20] = crhs[20:24]


def join_kernel(up, down, tcm, tcp, whole, tall):
    whole[0:16] = tcm[0:16]
    whole[12:16] = tcm[12:16] + down[16:20]
    whole[16:32] = up[0:16]
    whole[16:20] = up[0:4] + tcm[16:20]
    whole[28:32] = up[12:16] + tcp[16:20]
    whole[32:48] = tcp[0:16]
    whole[32:36] = tcp[0:4] + up[16:20]
    tall[...] = whole[4:44]


def diamond(radius):
    rows = []
    for t in range(-radius, 4 + radius):
        reach = radius - max(0, -t, t - 3)
        rows.append((t, -reach, 4 + 2 * reach))
    return rows


def coarse_kernel(
    whole, e2m, e2p, zcm, zcp, csmat, cmat, coarse_ref, prolong_ref,
    lifted,
    w0, w, packed, operand,
):
    for t in range(12):
        own = whole[4 * t : 4 * t + 4]
        if t in (0, 11):
            own = own + (e2p if t else e2m)[...]
        w[pl.ds(t * 12 + 4, 4)] = own
        side = t - 1
        if 0 <= side < 10:
            w[pl.ds(t * 12, 4)] = zcm[4 * side : 4 * side + 4]
            w[pl.ds(t * 12 + 8, 4)] = zcp[4 * side : 4 * side + 4]

    def spot(t, z):
        return (t + 4) * 12 + z + 4

    row = 0
    for t, z, count in diamond(4):
        size = count * CP
        top, tail = halves(w[pl.ds(spot(t, z), count)].reshape(size, CC))
        packed[row : row + size, 0:CC] = top
        packed[row : row + size, CC : 2 * CC] = tail
        row += size
    both = dot(packed[...], csmat[...])
    first = both[:, 0:CC] + both[:, CC : 2 * CC]
    row = 0
    for t, z, count in diamond(4):
        size = count * CP
        value = first[row : row + size].reshape(count, CP, CC)
        w0[pl.ds(spot(t, z), count)] = value
        w[pl.ds(spot(t, z), count)] = value
        row += size
    turn = [coarse_ref[hop] for hop in range(4)]

    for sweep in range(SWEEPS):
        shape = diamond(SWEEPS - sweep)
        row = 0
        for t, z, count in shape:
            size = count * CP
            start = spot(t, z)
            blocks = [w[pl.ds(start + offset, count)].reshape(size, CC) for offset in (0, 12, -12, 1, -1)]
            for hop in range(4):
                blocks.append(
                    jnp.concatenate(
                        [jnp.take_along_axis(w[start + n], turn[hop], axis=0) for n in range(count)], axis=0
                    )
                )
            for hop, block in enumerate(blocks):
                top, tail = halves(block)
                operand[row : row + size, hop * CC : (hop + 1) * CC] = top
                operand[row : row + size, KC + hop * CC : KC + (hop + 1) * CC] = tail
            row += size
        both = dot(operand[0:row, :], cmat[...])
        change = both[:, 0:CC] + both[:, CC : 2 * CC]
        row = 0
        for t, z, count in shape:
            size = count * CP
            place_of = pl.ds(spot(t, z), count)
            w[place_of] = w[place_of] + w0[place_of] - change[row : row + size].reshape(count, CP, CC)
            row += size

    near = jnp.concatenate([w[pl.ds(spot(t, -1), 6)] for t in range(-1, 5)], axis=0)
    near = jnp.concatenate([near.reshape(36 * CP, CC), jnp.zeros((12 * CP, CC), F32)], axis=0)
    top, tail = halves(near)
    ptop, ptail = halves(prolong_ref[...])
    up = dot_nt(ptop, top) + dot_nt(ptop, tail) + dot_nt(ptail, top)
    for part in range(3):
        lifted[part] = up[:, part * PL : (part + 1) * PL]


def correct_kernel(
    lifted, lift_ref, plane_ref, x1, xm, xp, x0, lw, mmat,
    field, wide, first, last,
    vhigh, vlow,
):
    plane = plane_tables(plane_ref)
    home = jnp.broadcast_to(lift_ref[0:1, :], (CF, PL))

    def raised(t, z):
        number = (t + 1) * 6 + z + 1
        return lanes_of(lifted[lax.div(number, 16)], home + CP * lax.rem(number, 16))

    def correct(index, carry):
        t, z = lax.div(index, 3), 2 * lax.rem(index, 3) - 1
        for column in range(2):
            site = place(t, z) + column
            field[site] = x1[site] + raised(t, z + column)
        return carry

    lax.fori_loop(0, 12, correct, 0)

    def correct_outside(z, carry):
        field[place(-1, z)] = xm[z] + raised(-1, z)
        field[place(4, z)] = xp[z] + raised(4, z)
        return carry

    lax.fori_loop(0, 4, correct_outside, 0)

    def finish(t, half, changes):
        for column, change in enumerate(changes):
            site = place(t, 2 * half + column)
            new = field[site] + x0[site] - change
            wide[site] = new
            (last if t else first)[2 * half + column] = new

    block_pairs((0, 3), mmat, field, lw, plane, vhigh, vlow, finish)


def rest_kernel(
    field, wide_in, first, last, plane_ref, x0, lw, mmat,
    wide, second, third, zlow, zhigh,
    vhigh, vlow,
):
    plane = plane_tables(plane_ref)
    halves_in_z = (zlow, zhigh)
    for half, target in enumerate(halves_in_z):
        target[0:2] = first[2 * half : 2 * half + 2]
        target[6:8] = last[2 * half : 2 * half + 2]

    def finish(t, half, changes):
        for column, change in enumerate(changes):
            site = place(t, 2 * half + column)
            new = field[site] + x0[site] - change
            wide[site] = new
            (second if t == 1 else third)[2 * half + column] = new
            halves_in_z[half][2 * t + column] = new

    block_pairs((1, 2), mmat, field, lw, plane, vhigh, vlow, finish)


def inner_kernel(wide_in, hzm, hzp, x0, lw, mmat, plane_ref, wide, x4, vhigh, vlow):
    plane = plane_tables(plane_ref)
    for t in range(4):
        wide[pl.ds(place(t, -2), 2)] = hzm[2 * t : 2 * t + 2]
        wide[pl.ds(place(t, 4), 2)] = hzp[2 * t : 2 * t + 2]

    blank_rows(wide, -1, 6)
    sweeps(6, edge_pair, mmat, wide, x0, lw, plane, vhigh, vlow, x4)
    sweeps(6, middle_pair, mmat, wide, x0, lw, plane, vhigh, vlow, x4)


def post_kernel(
    wide_in, x4_in, tm1, tm2, tp1, tp2, czm, czp, a0, a1, a2, a3, x0, lw, mmat, bmat, mhops, plane_ref,
    wide, x4, sol_out, res_out,
    vhigh, vlow, rest, sems,
):
    plane = plane_tables(plane_ref)
    for source, t in ((tm1, -1), (tm2, -2), (tp1, 4), (tp2, 5)):
        wide[pl.ds(place(t, 0), 4)] = source[...]
    for source, z in ((czm, -1), (czp, 4)):
        wide[place(-1, z)] = source[0]
        wide[place(4, z)] = source[1]

    close_edges(mhops, wide, lw, vhigh, vlow, x4)
    sweeps(4, outer_pair, mmat, wide, x0, lw, plane, vhigh, vlow, x4)

    def send(source, target, number, kind):
        copy = pltpu.make_async_copy(source, target.at[:, number, :], sems.at[kind, number])
        copy.start()
        return copy

    copies = [send(x4.at[place(n // 4, n % 4)], sol_out, n, 0) for n in range(16)]
    rows = (a0, a1, a2, a3)

    def finish(t, half, images):
        for column, image in enumerate(images):
            number = 4 * t + 2 * half + column
            rest[number] = rows[t][2 * half + column] - image
            copies.append(send(rest.at[number], res_out, number, 1))

    block_pairs(range(4), bmat, x4, lw, plane, vhigh, vlow, finish)
    for copy in copies:
        copy.wait()


STACKED = ((2, KF, 2 * PL), BF16)
FRAME = ((64, CF, PL), F32)
WEIGHTS = ((64, 8, PL), F32)
ROW = ((4, CF, PL), F32)
PAIRED = ((2 * CF, KF), BF16)


def call(kernel, outs, scratch, aliases, *args, limit=8, far=()):
    vmem, away = pl.BlockSpec(memory_space=pltpu.VMEM), pl.BlockSpec(memory_space=pl.ANY)
    return pl.pallas_call(
        kernel,
        out_shape=tuple(jax.ShapeDtypeStruct(shape, kind) for shape, kind in outs),
        in_specs=[vmem] * len(args),
        out_specs=tuple(away if number in far else vmem for number in range(len(outs))),
        scratch_shapes=[
            pltpu.VMEM(*entry) if isinstance(entry, tuple) else entry for entry in scratch
        ],
        input_output_aliases=aliases,
        compiler_params=pltpu.CompilerParams(vmem_limit_bytes=limit << 20),
    )(*args)


def moved(value, axes, step):
    count = 1
    for axis in axes if isinstance(axes, tuple) else (axes,):
        count *= lax.axis_size(axis)
    return lax.ppermute(value, axes, [(i, (i + step) % count) for i in range(count)])


def shards(
    rhs_field,
    link_weights,
    fine_blocks,
    smoother,
    plane_next,
    aggregate,
    restrict_map,
    prolong_map,
    coarse_blocks,
    coarse_smoother,
    coarse_next,
):
    rows = [jnp.transpose(rhs_field[0, :, t], (1, 0, 2)) for t in range(4)]
    lows, highs = (
        jnp.concatenate(
            [
                jnp.transpose(rhs_field[0, :, :, z : z + 2], (1, 2, 0, 3)),
                jnp.transpose(link_weights[:, :, z : z + 2], (1, 2, 0, 3)),
            ],
            axis=2,
        ).reshape(8, CF + 8, PL)
        for z in (0, 2)
    )
    ends = [
        jnp.concatenate([rows[t], jnp.transpose(link_weights[:, t], (1, 0, 2))], axis=1) for t in (0, 3)
    ]
    hzm, hzp = moved(highs, "gz", 1), moved(lows, "gz", -1)
    tm1, tp1 = moved(ends[1], TAXES, 1), moved(ends[0], TAXES, -1)
    ctm = moved(jnp.stack([hzm[7, 0:CF], hzp[6, 0:CF]]), TAXES, 1)
    ctp = moved(jnp.stack([hzm[1, 0:CF], hzp[0, 0:CF]]), TAXES, -1)

    hops = ((2, 2 * CF, CF), BF16)
    smat, mpair, bpair, cpair, csmat, mhops, bhops = call(
        prepare_kernel,
        (
            ((2 * CF, CF), BF16),
            PAIRED,
            PAIRED,
            ((2 * KC, 2 * CC), BF16),
            ((2 * CC, 2 * CC), BF16),
            hops,
            hops,
        ),
        (),
        {},
        smoother, fine_blocks, coarse_smoother, coarse_blocks,
    )
    member = (jnp.arange(16, dtype=jnp.int32)[:, None] == aggregate[None, :]).astype(F32)
    turn = jnp.broadcast_to(coarse_next[:, :, None], (4, CP, CC))
    home = jnp.broadcast_to(aggregate[None, :], (8, PL))

    x0, lw, x1 = call(
        local_kernel,
        (FRAME, WEIGHTS, FRAME),
        (STACKED, STACKED),
        {},
        *rows, link_weights.reshape(8, 16, PL), hzm, hzp, smat, mpair, plane_next,
    )
    (x1,) = call(edge_kernel, (FRAME,), (STACKED, STACKED), {2: 0}, x0, lw, x1, mpair, plane_next)
    x0, lw, x1, up, down, first, last = call(
        pre_kernel,
        (FRAME, WEIGHTS, FRAME, ((20, CP, CC), F32), ((20, CP, CC), F32), ROW, ROW),
        (STACKED, STACKED, ((24 * CP, CF), F32)),
        {15: 0, 16: 1, 17: 2},
        *rows, tm1, tp1, ctm, ctp, smat, bpair, mhops, bhops, restrict_map, plane_next, member,
        x0, lw, x1,
    )

    tcm, tcp = moved(up, TAXES, 1), moved(down, TAXES, -1)
    e2m, e2p = moved(up[16:20], TAXES, 2), moved(down[16:20], TAXES, -2)
    whole, tall = call(
        join_kernel,
        (((48, CP, CC), F32), ((40, CP, CC), F32)),
        (),
        {},
        up, down, tcm, tcp,
    )
    zcm, zcp = moved(tall, "gz", 1), moved(tall, "gz", -1)
    xm, xp = moved(last, TAXES, 1), moved(first, TAXES, -1)

    (lifted,) = call(
        coarse_kernel,
        (((3, CF, PL), F32),),
        (
            ((144, CP, CC), F32),
            ((144, CP, CC), F32),
            ((104 * CP, 2 * CC), BF16),
            ((76 * CP, 2 * KC), BF16),
        ),
        {},
        whole, e2m, e2p, zcm, zcp, csmat, cpair, turn, prolong_map.T,
        limit=12,
    )
    field, wide, r0, r3 = call(
        correct_kernel,
        (FRAME, FRAME, ROW, ROW),
        (STACKED, STACKED),
        {},
        lifted, home, plane_next, x1, xm, xp, x0, lw, mpair,
    )
    half = ((8, CF, PL), F32)
    wide, r1, r2, low, high = call(
        rest_kernel,
        (FRAME, ROW, ROW, half, half),
        (STACKED, STACKED),
        {1: 0},
        field, wide, r0, r3, plane_next, x0, lw, mpair,
    )
    tm1, tp1 = moved(r3, TAXES, 1), moved(r0, TAXES, -1)
    tm2, tp2 = moved(r2, TAXES, 1), moved(r1, TAXES, -1)
    hzm, hzp = moved(high, "gz", 1), moved(low, "gz", -1)
    czm = moved(jnp.stack([tm1[3], tp1[3]]), "gz", 1)
    czp = moved(jnp.stack([tm1[0], tp1[0]]), "gz", -1)
    wide, x4 = call(
        inner_kernel,
        (FRAME, FRAME),
        (STACKED, STACKED),
        {0: 0},
        wide, hzm, hzp, x0, lw, mpair, plane_next,
    )
    _, _, sol, res = call(
        post_kernel,
        (FRAME, FRAME, ((CF, 16, PL), F32), ((CF, 16, PL), F32)),
        (STACKED, STACKED, ((16, CF, PL), F32), pltpu.SemaphoreType.DMA((2, 16))),
        {0: 0, 1: 1},
        wide, x4, tm1, tm2, tp1, tp2, czm, czp, *rows, x0, lw, mpair, bpair, mhops, plane_next,
        far=(2, 3),
    )

    def natural(value):
        return value.reshape(1, CF, 4, 4, PL)

    return natural(sol), natural(res)


def solution(mesh):
    spread = P(None, None, TAXES, "gz", None)
    return jax.shard_map(
        shards,
        mesh=mesh,
        in_specs=(spread, P(None, TAXES, "gz", None)) + (P(),) * 9,
        out_specs=(spread, spread),
        check_vma=False,
    )
```

profile of v0, /device:TPU:0, one launch (start us, length us, event | category | flops | bytes accessed | tf_op | source)
XLA Modules:
  0.0 99.4 jit_solution(9273388186074961999)
XLA Ops:
  0.6 0.0 copy-start.8
  0.7 1.0 %slice_bitcast_fusion.3 = (f32[4,2,8,128]{3,1,0,2:T(2,128)S(1)}, f32[4,2,8,128]{3,1,0,2:T(2,128)S(1)}) fusion(f32[8,4,4,128]{3,2,1,0:T(4,128)} %param.12), kind=kLoop, calls=%fused_computation.15 | loop fusion | bytes 131072 | tf_op jit(solution)/shard_map/transpose | solution.py:518
  1.7 1.7 %slice_bitcast_fusion.1 = (f32[4,2,96,128]{3,1,0,2:T(2,128)S(1)}, f32[4,2,96,128]{3,1,0,2:T(2,128)S(1)}) fusion(f32[1,96,4,4,128]{4,3,2,1,0:T(4,128)} %param.11), kind=kLoop, calls=%fused_computation.3 | loop fusion | bytes 1572864 | tf_op jit(solution)/shard_map/transpose | solution.py:517
  3.4 0.4 pad_maximum_fusion
  3.8 0.0 copy-start.10
  3.8 0.0 copy-start
  3.8 0.0 copy-start.1
  3.8 0.0 copy-start.4
  3.9 0.0 copy-start.6
  3.9 0.1 copy.28
  4.0 3.6 %collective-permute-start.3 = (f32[8,104,128]{2,1,0:T(8,128)S(1)}, f32[8,104,128]{2,1,0:T(8,128)S(1)}, u32[]{:S(2)}, u32[]{:S(2)}) collective-permute-start(f32[8,104,128]{2,1,0:T(8,128)S(1)} %bitcast.56), channel_id=1, source_target_pairs={{0,14},{2,0},{4,2},{6,4},{8,6},{10,8},{12,10},{14,12},{1,15},{3,1}... | collective-permute-start | bytes 1277960 | tf_op jit(solution)/shard_map/ppermute | solution.py:497
  7.6 0.0 copy-start.3
  7.6 0.1 fusion.1
  7.8 5.3 %collective-permute-start.1 = (f32[4,104,128]{2,1,0:T(8,128)S(1)}, f32[4,104,128]{2,1,0:T(8,128)S(1)}, u32[]{:S(2)}, u32[]{:S(2)}) collective-permute-start(f32[4,104,128]{2,1,0:T(8,128)S(1)} %pad_maximum_fusion.3), channel_id=1, source_target_pairs={{0,113},{1,0},{16,1},{17,16},{32,17},{33,32},{48,33},{49,48},{64,4... | collective-permute-start | bytes 638984 | tf_op jit(solution)/shard_map/ppermute | solution.py:497
  13.1 0.1 collective-permute-start
  13.2 0.1 copy.27
  13.3 0.0 collective-permute-start.2
  13.4 8.7 %collective-permute-done.2.hzm = f32[8,104,128]{2,1,0:T(8,128)S(1)} collective-permute-done((f32[8,104,128]{2,1,0:T(8,128)S(1)}, f32[8,104,128]{2,1,0:T(8,128)S(1)}, u32[]{:S(2)}, u32[]{:S(2)}) %collective-permute-start.2) | collective-permute-done | bytes 426016 | tf_op jit(solution)/shard_map/ppermute | solution.py:497
  22.1 2.5 %collective-permute-start.4 = (f32[2,96,128]{2,1,0:T(8,128)S(1)}, f32[2,96,128]{2,1,0:T(8,128)S(1)}, u32[]{:S(2)}, u32[]{:S(2)}) collective-permute-start(f32[2,96,128]{2,1,0:T(8,128)S(1)} %pad_maximum_fusion.4), channel_id=1, source_target_pairs={{0,1},{1,16},{16,17},{17,32},{32,33},{33,48},{48,49},{49,64},{64,6... | collective-permute-start | bytes 294920 | tf_op jit(solution)/shard_map/ppermute | solution.py:497
  24.6 3.0 %collective-permute-start.5 = (f32[2,96,128]{2,1,0:T(8,128)S(1)}, f32[2,96,128]{2,1,0:T(8,128)S(1)}, u32[]{:S(2)}, u32[]{:S(2)}) collective-permute-start(f32[2,96,128]{2,1,0:T(8,128)S(1)} %pad_maximum_fusion.5), channel_id=1, source_target_pairs={{0,113},{1,0},{16,1},{17,16},{32,17},{33,32},{48,33},{49,48},{64,4... | collective-permute-start | bytes 294920 | tf_op jit(solution)/shard_map/ppermute | solution.py:497
  27.6 1.2 %shard_map.122 = (bf16[192,96]{1,0:T(8,128)(2,1)S(1)}, bf16[192,864]{1,0:T(8,128)(2,1)S(1)}, bf16[192,864]{1,0:T(8,128)(2,1)S(1)}, bf16[2304,256]{1,0:T(8,128)(2...) custom-call(f32[96,96]{1,0:T(8,128)S(1)} %copy-done.6, ...), custom_call_target="tpu_custom_call" | custom-call | tf_op jit(solution)/shard_map/pallas_call | solution.py:480
  28.9 2.8 %shard_map.123 = (f32[64,96,128]{2,1,0:T(8,128)S(1)}, f32[64,8,128]{2,1,0:T(8,128)S(1)}, f32[64,96,128]{2,1,0:T(8,128)S(1)}) custom-call(f32[4,96,128]{2,1,0:T(8,128)S(1)} %bitcast.47, f32[4,96,128]{2,1,0:T(8,128)S(1)} %get-tuple-element.85.a1, f32[4,96,128]{2,1,0:T(8,128)S(1)} %get-tuple-element.84.a2, f32[4,96,128]{2,1,0:T(8,128)S(1)} %bitcast.51, ...), custom_call_target="tpu_custom_call" | custom-call | tf_op jit(solution)/shard_map/pallas_call | solution.py:480
  31.8 0.0 copy-start.5
  31.8 2.1 %shard_map.124.x1_in = f32[64,96,128]{2,1,0:T(8,128)S(1)} custom-call(f32[64,96,128]{2,1,0:T(8,128)S(1)} %get-tuple-element.39.x0.x0_in, f32[64,8,128]{2,1,0:T(8,128)S(1)} %get-tuple-element.40.lw.lw_in, f32[64,96,128]{2,1,0:T(8,128)S(1)} %get-tuple-element.41.x1_in, bf16[192,864]{1,0:T(8,128)(2,1)S(1)} %get-tuple-element.38.mmat, ...), custom_call_target="tpu_custom_call", output_to_operand_aliasing={{}: (2, {})} | custom-call | tf_op jit(solution)/shard_map/pallas_call | solution.py:480
  33.9 0.0 collective-permute-done.tm1
  33.9 0.0 copy-start.9
  34.0 0.0 copy-start.7
  34.0 7.0 %shard_map.125 = (f32[64,96,128]{2,1,0:T(8,128)S(1)}, f32[64,8,128]{2,1,0:T(8,128)S(1)}, f32[64,96,128]{2,1,0:T(8,128)S(1)}, f32[20,8,128]{2,1,0:T(8,128)S(1)}, ...) custom-call(f32[4,96,128]{2,1,0:T(8,128)S(1)} %bitcast.48, ...), custom_call_target="tpu_custom_call", output_to_operand_aliasing={{0}: (15, {}), {1}: (16, {}), {2}: (17, {})} | custom-call | tf_op jit(solution)/shard_map/pallas_call | solution.py:480
  41.0 0.8 collective-permute-start.6
  41.8 4.8 %collective-permute-start.7 = (f32[20,8,128]{2,1,0:T(8,128)S(1)}, f32[20,8,128]{2,1,0:T(8,128)S(1)}, u32[]{:S(2)}, u32[]{:S(2)}) collective-permute-start(f32[20,8,128]{2,1,0:T(8,128)S(1)} %get-tuple-element.43.down), channel_id=1, source_target_pairs={{0,113},{1,0},{16,1},{17,16},{32,17},{33,32},{48,33},{49,48},{64,4... | collective-permute-start | bytes 245768 | tf_op jit(solution)/shard_map/ppermute | solution.py:497
  46.6 5.3 %collective-permute-start.13 = (f32[4,96,128]{2,1,0:T(8,128)S(1)}, f32[4,96,128]{2,1,0:T(8,128)S(1)}, u32[]{:S(2)}, u32[]{:S(2)}) collective-permute-start(f32[4,96,128]{2,1,0:T(8,128)S(1)} %get-tuple-element.50), channel_id=1, source_target_pairs={{0,113},{1,0},{16,1},{17,16},{32,17},{33,32},{48,33},{49,48},{64,4... | collective-permute-start | bytes 589832 | tf_op jit(solution)/shard_map/ppermute | solution.py:497
  51.9 0.0 collective-permute-start.11
  52.0 0.5 collective-permute-start.10
  52.5 3.7 %collective-permute-done.9.e2p = f32[4,8,128]{2,1,0:T(8,128)S(1)} collective-permute-done((f32[4,8,128]{2,1,0:T(8,128)S(1)}, f32[4,8,128]{2,1,0:T(8,128)S(1)}, u32[]{:S(2)}, u32[]{:S(2)}) %collective-permute-start.9) | collective-permute-done | bytes 16416 | tf_op jit(solution)/shard_map/ppermute | solution.py:497
  56.2 5.8 %collective-permute-done.8.e2m = f32[4,8,128]{2,1,0:T(8,128)S(1)} collective-permute-done((f32[4,8,128]{2,1,0:T(8,128)S(1)}, f32[4,8,128]{2,1,0:T(8,128)S(1)}, u32[]{:S(2)}, u32[]{:S(2)}) %collective-permute-start.8) | collective-permute-done | bytes 16416 | tf_op jit(solution)/shard_map/ppermute | solution.py:497
  62.1 0.1 broadcast_in_dim.4.coarse_ref
  62.1 4.0 %shard_map.127.lifted = f32[3,96,128]{2,1,0:T(8,128)S(1)} custom-call(f32[48,8,128]{2,1,0:T(8,128)S(1)} %get-tuple-element.44.whole, f32[4,8,128]{2,1,0:T(8,128)S(1)} %collective-permute-done.8.e2m, f32[4,8,128]{2,1,0:T(8,128)S(1)} %collective-permute-done.9.e2p, f32[40,8,128]{2,1,0:T(8,128)S(1)} %collective-permute-done.10.zcm, ...), custom_call_target="tpu_custom_call" | custom-call | tf_op jit(solution)/shard_map/pallas_call | solution.py:480
  66.2 3.2 %shard_map.128 = (f32[64,96,128]{2,1,0:T(8,128)S(1)}, f32[64,96,128]{2,1,0:T(8,128)S(1)}, f32[4,96,128]{2,1,0:T(8,128)S(1)}, f32[4,96,128]{2,1,0:T(8,128)S(1)}) custom-call(f32[3,96,128]{2,1,0:T(8,128)S(1)} %shard_map.127.lifted, s32[8,128]{1,0:T(8,128)S(1)} %broadcast_in_dim.5.lift_ref, s32[4,128]{1,0:T(4,128)S(1)} %copy-done.3, ...), custom_call_target="tpu_custom_call" | custom-call | tf_op jit(solution)/shard_map/pallas_call | solution.py:480
  69.4 3.8 %collective-permute-start.18 = (f32[4,96,128]{2,1,0:T(8,128)S(1)}, f32[4,96,128]{2,1,0:T(8,128)S(1)}, u32[]{:S(2)}, u32[]{:S(2)}) collective-permute-start(f32[4,96,128]{2,1,0:T(8,128)S(1)} %get-tuple-element.55.first), channel_id=1, source_target_pairs={{0,113},{1,0},{16,1},{17,16},{32,17},{33,32},{48,33},{49,48},{64,4... | collective-permute-start | bytes 589832 | tf_op jit(solution)/shard_map/ppermute | solution.py:497
  73.3 1.6 %shard_map.129 = (f32[64,96,128]{2,1,0:T(8,128)S(1)}, f32[4,96,128]{2,1,0:T(8,128)S(1)}, f32[4,96,128]{2,1,0:T(8,128)S(1)}, f32[8,96,128]{2,1,0:T(8,128)S(1)}, f32[8,96,128]{2,1,0:T(8,128)S(1)}) custom-call(f32[64,96,128]{2,1,0:T(8,128)S(1)} %get-tuple-element.53.field, ...), custom_call_target="tpu_custom_call", output_to_operand_aliasing={{0}: (1, {})} | custom-call | tf_op jit(solution)/shard_map/pallas_call | solution.py:480
  74.8 3.9 %collective-permute-start.17 = (f32[4,96,128]{2,1,0:T(8,128)S(1)}, f32[4,96,128]{2,1,0:T(8,128)S(1)}, u32[]{:S(2)}, u32[]{:S(2)}) collective-permute-start(f32[4,96,128]{2,1,0:T(8,128)S(1)} %get-tuple-element.62), channel_id=1, source_target_pairs={{0,1},{1,16},{16,17},{17,32},{32,33},{33,48},{48,49},{49,64},{64,6... | collective-permute-start | bytes 589832 | tf_op jit(solution)/shard_map/ppermute | solution.py:497
  78.8 1.8 %collective-permute-start.19 = (f32[4,96,128]{2,1,0:T(8,128)S(1)}, f32[4,96,128]{2,1,0:T(8,128)S(1)}, u32[]{:S(2)}, u32[]{:S(2)}) collective-permute-start(f32[4,96,128]{2,1,0:T(8,128)S(1)} %get-tuple-element.63), channel_id=1, source_target_pairs={{0,113},{1,0},{16,1},{17,16},{32,17},{33,32},{48,33},{49,48},{64,4... | collective-permute-start | bytes 589832 | tf_op jit(solution)/shard_map/ppermute | solution.py:497
  80.6 3.0 %collective-permute-start.15 = (f32[8,96,128]{2,1,0:T(8,128)S(1)}, f32[8,96,128]{2,1,0:T(8,128)S(1)}, u32[]{:S(2)}, u32[]{:S(2)}) collective-permute-start(f32[8,96,128]{2,1,0:T(8,128)S(1)} %get-tuple-element.59), channel_id=1, source_target_pairs={{0,14},{2,0},{4,2},{6,4},{8,6},{10,8},{12,10},{14,12},{1,15},{3,1}... | collective-permute-start | bytes 1179656 | tf_op jit(solution)/shard_map/ppermute | solution.py:497
  83.5 1.7 %collective-permute-done.16.tm1 = f32[4,96,128]{2,1,0:T(8,128)S(1)} collective-permute-done((f32[4,96,128]{2,1,0:T(8,128)S(1)}, f32[4,96,128]{2,1,0:T(8,128)S(1)}, u32[]{:S(2)}, u32[]{:S(2)}) %collective-permute-start.16) | collective-permute-done | bytes 196640 | tf_op jit(solution)/shard_map/ppermute | solution.py:497
  85.3 0.0 collective-permute-start.20
  85.3 3.6 %collective-permute-done.14.hzm = f32[8,96,128]{2,1,0:T(8,128)S(1)} collective-permute-done((f32[8,96,128]{2,1,0:T(8,128)S(1)}, f32[8,96,128]{2,1,0:T(8,128)S(1)}, u32[]{:S(2)}, u32[]{:S(2)}) %collective-permute-start.14) | collective-permute-done | bytes 393248 | tf_op jit(solution)/shard_map/ppermute | solution.py:497
  89.0 4.1 %shard_map.130 = (f32[64,96,128]{2,1,0:T(8,128)S(1)}, f32[64,96,128]{2,1,0:T(8,128)S(1)}) custom-call(f32[64,96,128]{2,1,0:T(8,128)S(1)} %get-tuple-element.57.wide_in, f32[8,96,128]{2,1,0:T(8,128)S(1)} %collective-permute-done.14.hzm, f32[8,96,128]{2,1,0:T(8,128)S(1)} %collective-permute-done.15.hzp, ...), custom_call_target="tpu_custom_call", output_to_operand_aliasing={{0}: (0, {})} | custom-call | tf_op jit(solution)/shard_map/pallas_call | solution.py:480
  93.2 6.0 %shard_map.131 = (f32[64,96,128]{2,1,0:T(8,128)S(1)}, f32[64,96,128]{2,1,0:T(8,128)S(1)}, f32[96,16,128]{2,1,0:T(8,128)}, f32[96,16,128]{2,1,0:T(8,128)}) custom-call(f32[64,96,128]{2,1,0:T(8,128)S(1)} %get-tuple-element.60.wide_in, f32[64,96,128]{2,1,0:T(8,128)S(1)} %get-tuple-element.61.x4_in, ...), custom_call_target="tpu_custom_call", output_to_operand_aliasing={{0}: (0, {}), {1}: (1, {})} | custom-call | tf_op jit(solution)/shard_map/pallas_call | solution.py:480
  (55 shorter events, 0.3 us)
Async XLA Ops:
  0.6 6.9 %copy-start.2 = (f32[8,4,4,128]{3,2,1,0:T(4,128)S(1)}, f32[8,4,4,128]{3,2,1,0:T(4,128)}, u32[]{:S(2)}) copy-start(f32[8,4,4,128]{3,2,1,0:T(4,128)} %param.12) | copy-start | bytes 196612
  0.6 6.9 %copy-start.8 = (f32[1,96,4,4,128]{4,3,2,1,0:T(4,128)S(1)}, f32[1,96,4,4,128]{4,3,2,1,0:T(4,128)}, u32[]{:S(2)}) copy-start(f32[1,96,4,4,128]{4,3,2,1,0:T(4,128)} %param.11) | copy-start | bytes 2359300
  3.8 23.8 %copy-start.10 = (s32[128]{0:T(128)S(1)}, s32[128]{0:T(128)}, u32[]{:S(2)}) copy-start(s32[128]{0:T(128)} %param.16) | copy-start | bytes 1540
  3.8 23.8 %copy-start = (f32[9,128,128]{2,1,0:T(8,128)S(1)}, f32[9,128,128]{2,1,0:T(8,128)}, u32[]{:S(2)}) copy-start(f32[9,128,128]{2,1,0:T(8,128)} %coarse.1) | copy-start | bytes 1769476
  3.8 23.8 %copy-start.1 = (f32[9,96,96]{2,1,0:T(8,128)S(1)}, f32[9,96,96]{2,1,0:T(8,128)}, u32[]{:S(2)}) copy-start(f32[9,96,96]{2,1,0:T(8,128)} %blocks.1) | copy-start | bytes 995332
  3.8 23.8 %copy-start.4 = (f32[128,128]{1,0:T(8,128)S(1)}, f32[128,128]{1,0:T(8,128)}, u32[]{:S(2)}) copy-start(f32[128,128]{1,0:T(8,128)} %cs_ref.1) | copy-start | bytes 196612
  3.9 23.8 %copy-start.6 = (f32[96,96]{1,0:T(8,128)S(1)}, f32[96,96]{1,0:T(8,128)}, u32[]{:S(2)}) copy-start(f32[96,96]{1,0:T(8,128)} %s_ref.1) | copy-start | bytes 110596
  4.0 9.4 %collective-permute-start.3 = (f32[8,104,128]{2,1,0:T(8,128)S(1)}, f32[8,104,128]{2,1,0:T(8,128)S(1)}, u32[]{:S(2)}, u32[]{:S(2)}) collective-permute-start(f32[8,104,128]{2,1,0:T(8,128)S(1)} %bitcast.56), channel_id=1, source_target_pairs={{0,14},{2,0},{4,2},{6,4},{8,6},{10,8},{12,10},{14,12},{1,15},{3,1}... | collective-permute-start | bytes 1277960 | tf_op jit(solution)/shard_map/ppermute | solution.py:497
  7.6 21.3 %copy-start.3 = (s32[4,128]{1,0:T(4,128)S(1)}, s32[4,128]{1,0:T(4,128)}, u32[]{:S(2)}) copy-start(s32[4,128]{1,0:T(4,128)} %plane_ref.13) | copy-start | bytes 6148
  7.8 26.1 %collective-permute-start.1 = (f32[4,104,128]{2,1,0:T(8,128)S(1)}, f32[4,104,128]{2,1,0:T(8,128)S(1)}, u32[]{:S(2)}, u32[]{:S(2)}) collective-permute-start(f32[4,104,128]{2,1,0:T(8,128)S(1)} %pad_maximum_fusion.3), channel_id=1, source_target_pairs={{0,113},{1,0},{16,1},{17,16},{32,17},{33,32},{48,33},{49,48},{64,4... | collective-permute-start | bytes 638984 | tf_op jit(solution)/shard_map/ppermute | solution.py:497
  13.1 20.8 %collective-permute-start = (f32[4,104,128]{2,1,0:T(8,128)S(1)}, f32[4,104,128]{2,1,0:T(8,128)S(1)}, u32[]{:S(2)}, u32[]{:S(2)}) collective-permute-start(f32[4,104,128]{2,1,0:T(8,128)S(1)} %pad_maximum_fusion.2), channel_id=1, source_target_pairs={{0,1},{1,16},{16,17},{17,32},{32,33},{33,48},{48,49},{49,64},{64,6... | collective-permute-start | bytes 638984 | tf_op jit(solution)/shard_map/ppermute | solution.py:497
  13.3 8.8 %collective-permute-start.2 = (f32[8,104,128]{2,1,0:T(8,128)S(1)}, f32[8,104,128]{2,1,0:T(8,128)S(1)}, u32[]{:S(2)}, u32[]{:S(2)}) collective-permute-start(f32[8,104,128]{2,1,0:T(8,128)S(1)} %bitcast.57), channel_id=1, source_target_pairs={{0,2},{2,4},{4,6},{6,8},{8,10},{10,12},{12,14},{14,0},{1,3},{3,5},... | collective-permute-start | bytes 1277960 | tf_op jit(solution)/shard_map/ppermute | solution.py:497
  22.1 11.8 %collective-permute-start.4 = (f32[2,96,128]{2,1,0:T(8,128)S(1)}, f32[2,96,128]{2,1,0:T(8,128)S(1)}, u32[]{:S(2)}, u32[]{:S(2)}) collective-permute-start(f32[2,96,128]{2,1,0:T(8,128)S(1)} %pad_maximum_fusion.4), channel_id=1, source_target_pairs={{0,1},{1,16},{16,17},{17,32},{32,33},{33,48},{48,49},{49,64},{64,6... | collective-permute-start | bytes 294920 | tf_op jit(solution)/shard_map/ppermute | solution.py:497
  24.6 9.4 %collective-permute-start.5 = (f32[2,96,128]{2,1,0:T(8,128)S(1)}, f32[2,96,128]{2,1,0:T(8,128)S(1)}, u32[]{:S(2)}, u32[]{:S(2)}) collective-permute-start(f32[2,96,128]{2,1,0:T(8,128)S(1)} %pad_maximum_fusion.5), channel_id=1, source_target_pairs={{0,113},{1,0},{16,1},{17,16},{32,17},{33,32},{48,33},{49,48},{64,4... | collective-permute-start | bytes 294920 | tf_op jit(solution)/shard_map/ppermute | solution.py:497
  31.8 2.2 %copy-start.5 = (f32[96,128]{1,0:T(8,128)S(1)}, f32[96,128]{1,0:T(8,128)}, u32[]{:S(2)}) copy-start(f32[96,128]{1,0:T(8,128)} %r_ref.1) | copy-start | bytes 147460
  33.9 28.1 %copy-start.9 = (s32[4,8]{1,0:T(4,128)S(1)}, s32[4,8]{1,0:T(4,128)}, u32[]{:S(2)}) copy-start(s32[4,8]{1,0:T(4,128)} %param.21) | copy-start | bytes 388
  34.0 28.2 %copy-start.7 = (f32[128,96]{0,1:T(8,128)S(1)}, f32[128,96]{0,1:T(8,128)}, u32[]{:S(2)}) copy-start(f32[128,96]{0,1:T(8,128)} %param.18) | copy-start | bytes 147460
  41.0 10.9 %collective-permute-start.6 = (f32[20,8,128]{2,1,0:T(8,128)S(1)}, f32[20,8,128]{2,1,0:T(8,128)S(1)}, u32[]{:S(2)}, u32[]{:S(2)}) collective-permute-start(f32[20,8,128]{2,1,0:T(8,128)S(1)} %get-tuple-element.42.up), channel_id=1, source_target_pairs={{0,1},{1,16},{16,17},{17,32},{32,33},{33,48},{48,49},{49,64},{64,6... | collective-permute-start | bytes 245768 | tf_op jit(solution)/shard_map/ppermute | solution.py:497
  41.8 10.1 %collective-permute-start.7 = (f32[20,8,128]{2,1,0:T(8,128)S(1)}, f32[20,8,128]{2,1,0:T(8,128)S(1)}, u32[]{:S(2)}, u32[]{:S(2)}) collective-permute-start(f32[20,8,128]{2,1,0:T(8,128)S(1)} %get-tuple-element.43.down), channel_id=1, source_target_pairs={{0,113},{1,0},{16,1},{17,16},{32,17},{33,32},{48,33},{49,48},{64,4... | collective-permute-start | bytes 245768 | tf_op jit(solution)/shard_map/ppermute | solution.py:497
  46.6 19.6 %collective-permute-start.12 = (f32[4,96,128]{2,1,0:T(8,128)S(1)}, f32[4,96,128]{2,1,0:T(8,128)S(1)}, u32[]{:S(2)}, u32[]{:S(2)}) collective-permute-start(f32[4,96,128]{2,1,0:T(8,128)S(1)} %get-tuple-element.49), channel_id=1, source_target_pairs={{0,1},{1,16},{16,17},{17,32},{32,33},{33,48},{48,49},{49,64},{64,6... | collective-permute-start | bytes 589832 | tf_op jit(solution)/shard_map/ppermute | solution.py:497
  46.6 19.6 %collective-permute-start.13 = (f32[4,96,128]{2,1,0:T(8,128)S(1)}, f32[4,96,128]{2,1,0:T(8,128)S(1)}, u32[]{:S(2)}, u32[]{:S(2)}) collective-permute-start(f32[4,96,128]{2,1,0:T(8,128)S(1)} %get-tuple-element.50), channel_id=1, source_target_pairs={{0,113},{1,0},{16,1},{17,16},{32,17},{33,32},{48,33},{49,48},{64,4... | collective-permute-start | bytes 589832 | tf_op jit(solution)/shard_map/ppermute | solution.py:497
  51.9 10.1 %collective-permute-start.11 = (f32[40,8,128]{2,1,0:T(8,128)S(1)}, f32[40,8,128]{2,1,0:T(8,128)S(1)}, u32[]{:S(2)}, u32[]{:S(2)}) collective-permute-start(f32[40,8,128]{2,1,0:T(8,128)S(1)} %get-tuple-element.45), channel_id=1, source_target_pairs={{0,14},{2,0},{4,2},{6,4},{8,6},{10,8},{12,10},{14,12},{1,15},{3,1}... | collective-permute-start | bytes 491528 | tf_op jit(solution)/shard_map/ppermute | solution.py:497
  52.0 10.1 %collective-permute-start.10 = (f32[40,8,128]{2,1,0:T(8,128)S(1)}, f32[40,8,128]{2,1,0:T(8,128)S(1)}, u32[]{:S(2)}, u32[]{:S(2)}) collective-permute-start(f32[40,8,128]{2,1,0:T(8,128)S(1)} %get-tuple-element.45), channel_id=1, source_target_pairs={{0,2},{2,4},{4,6},{6,8},{8,10},{10,12},{12,14},{14,0},{1,3},{3,5},... | collective-permute-start | bytes 491528 | tf_op jit(solution)/shard_map/ppermute | solution.py:497
  52.5 3.7 %collective-permute-start.9 = (f32[4,8,128]{2,1,0:T(8,128)S(1)}, f32[4,8,128]{2,1,0:T(8,128)S(1)}, u32[]{:S(2)}, u32[]{:S(2)}) collective-permute-start(f32[4,8,128]{2,1,0:T(8,128)S(1)} %slice.75), channel_id=1, source_target_pairs={{0,112},{1,113},{16,0},{17,1},{32,16},{33,17},{48,32},{49,33},{64,... | collective-permute-start | bytes 49160 | tf_op jit(solution)/shard_map/ppermute | solution.py:497
  56.2 5.8 %collective-permute-start.8 = (f32[4,8,128]{2,1,0:T(8,128)S(1)}, f32[4,8,128]{2,1,0:T(8,128)S(1)}, u32[]{:S(2)}, u32[]{:S(2)}) collective-permute-start(f32[4,8,128]{2,1,0:T(8,128)S(1)} %slice.74), channel_id=1, source_target_pairs={{0,16},{1,17},{16,32},{17,33},{32,48},{33,49},{48,64},{49,65},{64,... | collective-permute-start | bytes 49160 | tf_op jit(solution)/shard_map/ppermute | solution.py:497
  69.4 11.1 %collective-permute-start.18 = (f32[4,96,128]{2,1,0:T(8,128)S(1)}, f32[4,96,128]{2,1,0:T(8,128)S(1)}, u32[]{:S(2)}, u32[]{:S(2)}) collective-permute-start(f32[4,96,128]{2,1,0:T(8,128)S(1)} %get-tuple-element.55.first), channel_id=1, source_target_pairs={{0,113},{1,0},{16,1},{17,16},{32,17},{33,32},{48,33},{49,48},{64,4... | collective-permute-start | bytes 589832 | tf_op jit(solution)/shard_map/ppermute | solution.py:497
  73.3 12.0 %collective-permute-start.16 = (f32[4,96,128]{2,1,0:T(8,128)S(1)}, f32[4,96,128]{2,1,0:T(8,128)S(1)}, u32[]{:S(2)}, u32[]{:S(2)}) collective-permute-start(f32[4,96,128]{2,1,0:T(8,128)S(1)} %get-tuple-element.56.last), channel_id=1, source_target_pairs={{0,1},{1,16},{16,17},{17,32},{32,33},{33,48},{48,49},{49,64},{64,6... | collective-permute-start | bytes 589832 | tf_op jit(solution)/shard_map/ppermute | solution.py:497
  74.8 18.3 %collective-permute-start.17 = (f32[4,96,128]{2,1,0:T(8,128)S(1)}, f32[4,96,128]{2,1,0:T(8,128)S(1)}, u32[]{:S(2)}, u32[]{:S(2)}) collective-permute-start(f32[4,96,128]{2,1,0:T(8,128)S(1)} %get-tuple-element.62), channel_id=1, source_target_pairs={{0,1},{1,16},{16,17},{17,32},{32,33},{33,48},{48,49},{49,64},{64,6... | collective-permute-start | bytes 589832 | tf_op jit(solution)/shard_map/ppermute | solution.py:497
  78.8 14.4 %collective-permute-start.19 = (f32[4,96,128]{2,1,0:T(8,128)S(1)}, f32[4,96,128]{2,1,0:T(8,128)S(1)}, u32[]{:S(2)}, u32[]{:S(2)}) collective-permute-start(f32[4,96,128]{2,1,0:T(8,128)S(1)} %get-tuple-element.63), channel_id=1, source_target_pairs={{0,113},{1,0},{16,1},{17,16},{32,17},{33,32},{48,33},{49,48},{64,4... | collective-permute-start | bytes 589832 | tf_op jit(solution)/shard_map/ppermute | solution.py:497
  80.5 8.4 %collective-permute-start.14 = (f32[8,96,128]{2,1,0:T(8,128)S(1)}, f32[8,96,128]{2,1,0:T(8,128)S(1)}, u32[]{:S(2)}, u32[]{:S(2)}) collective-permute-start(f32[8,96,128]{2,1,0:T(8,128)S(1)} %get-tuple-element.58), channel_id=1, source_target_pairs={{0,2},{2,4},{4,6},{6,8},{8,10},{10,12},{12,14},{14,0},{1,3},{3,5},... | collective-permute-start | bytes 1179656 | tf_op jit(solution)/shard_map/ppermute | solution.py:497
  80.6 8.4 %collective-permute-start.15 = (f32[8,96,128]{2,1,0:T(8,128)S(1)}, f32[8,96,128]{2,1,0:T(8,128)S(1)}, u32[]{:S(2)}, u32[]{:S(2)}) collective-permute-start(f32[8,96,128]{2,1,0:T(8,128)S(1)} %get-tuple-element.59), channel_id=1, source_target_pairs={{0,14},{2,0},{4,2},{6,4},{8,6},{10,8},{12,10},{14,12},{1,15},{3,1}... | collective-permute-start | bytes 1179656 | tf_op jit(solution)/shard_map/ppermute | solution.py:497
  85.3 7.8 %collective-permute-start.20 = (f32[2,96,128]{2,1,0:T(8,128)S(1)}, f32[2,96,128]{2,1,0:T(8,128)S(1)}, u32[]{:S(2)}, u32[]{:S(2)}) collective-permute-start(f32[2,96,128]{2,1,0:T(8,128)S(1)} %pad_maximum_fusion.6), channel_id=1, source_target_pairs={{0,2},{2,4},{4,6},{6,8},{8,10},{10,12},{12,14},{14,0},{1,3},{3,5},... | collective-permute-start | bytes 294920 | tf_op jit(solution)/shard_map/ppermute | solution.py:497
  89.0 4.2 %collective-permute-start.21 = (f32[2,96,128]{2,1,0:T(8,128)S(1)}, f32[2,96,128]{2,1,0:T(8,128)S(1)}, u32[]{:S(2)}, u32[]{:S(2)}) collective-permute-start(f32[2,96,128]{2,1,0:T(8,128)S(1)} %pad_maximum_fusion.7), channel_id=1, source_target_pairs={{0,14},{2,0},{4,2},{6,4},{8,6},{10,8},{12,10},{14,12},{1,15},{3,1}... | collective-permute-start | bytes 294920 | tf_op jit(solution)/shard_map/ppermute | solution.py:497
where the time goes:
time: 101 us; the launch traced here: 99.4 us
  starting transfers between devices  38.4 us (38%)
  Pallas kernels  32.2 us (32%)
  waiting for transfers between devices  23.7 us (23%)
  local copies, waits for them, and re-layouts  3.26 us (3%)
  between operations  1.28 us (1%)
    ppermute x22, starting transfers between devices, moved(): lax.ppermute(value, axes, [(i, (i + step) % count) for i in range(count)])  38.4 us
    pallas_call x10, Pallas kernels, call(): pl.pallas_call(kernel, out_shape=tuple((jax.ShapeDtypeStruct(shape, kind)...  32.2 us
    ppermute x22, waiting for transfers between devices, moved(): lax.ppermute(value, axes, [(i, (i + step) % count) for i in range(count)])  23.7 us
  transfers between devices with their start and end apart: 22, of which 5 were waited for; matrix products, arithmetic and copies ran while one was open for 0% of the time, Pallas kernels for 16%

commit v1 on v0

--- a/solution.py
+++ b/solution.py
@@ -30,16 +30,19 @@
     return jnp.take_along_axis(value, index, axis=1)
 
 
-def product(matrix, high, low):
-    both = dot(matrix[...], high[...])
-    return both[0:CF] + both[CF : 2 * CF] + dot(matrix[0:CF, :], low[...])
+def side_by_side(ref, depth):
+    return jnp.concatenate([ref[0, 0:depth, :], ref[1, 0:depth, :]], axis=1)
+
+
+def product(matrix, high, low, depth=KF):
+    both = dot(matrix[...], side_by_side(high, depth))
+    return both[0:CF] + both[CF : 2 * CF] + dot(matrix[0:CF, :], side_by_side(low, depth))
 
 
 def put(high, low, row, column, value):
     top, rest = halves(value)
-    rows, columns = pl.ds(row, CF), pl.ds(column * PL, PL)
-    high[rows, columns] = top
-    low[rows, columns] = rest
+    high[column, row : row + CF, :] = top
+    low[column, row : row + CF, :] = rest
 
 
 def fill(field, site, stride, weights, plane, high, low, column):
@@ -91,7 +94,7 @@
 def smooth(smat, high, low, x0, sources, targets):
     for column, source in enumerate(sources):
         put(high, low, 0, column, source)
-    value = product(smat, high.at[0:CF], low.at[0:CF])
+    value = product(smat, high, low, CF)
     for column, target in enumerate(targets):
         x0[target] = value[:, column * PL : (column + 1) * PL]
 
@@ -136,7 +139,7 @@
 def one_hop(matrix, values, vhigh, vlow, slot):
     for column, value in enumerate(values):
         put(vhigh.at[slot], vlow.at[slot], 0, column, value)
-    image = product(matrix, vhigh.at[slot, 0:CF], vlow.at[slot, 0:CF])
+    image = product(matrix, vhigh.at[slot], vlow.at[slot], CF)
     return [image[:, 0:PL], image[:, PL : 2 * PL]]
 
 
@@ -170,7 +173,22 @@
     target[depth + row : depth + row + CC, CC : 2 * CC] = jnp.zeros((CC, CC), BF16)
 
 
-def prepare_kernel(s_ref, blocks, cs_ref, coarse, smat, mmat, bmat, cmat, csmat, mhops, bhops):
+def prepare_kernel(
+    s_far, blocks_far, cs_far, coarse_far, r_far, prolong_far, plane_far, aggregate_far,
+    smat, mmat, bmat, cmat, csmat, mhops, bhops, restrict, prolong, plane, home, member,
+    s_ref, blocks, cs_ref, coarse, sems,
+):
+    copies = fetch(
+        (
+            (s_far, s_ref), (blocks_far, blocks), (cs_far, cs_ref), (coarse_far, coarse),
+            (r_far, restrict), (prolong_far, prolong), (plane_far, plane), (aggregate_far, home),
+        ),
+        sems,
+    )
+    for copy in copies:
+        copy.wait()
+    rows = lax.broadcasted_iota(jnp.int32, (16, PL), 0)
+    member[...] = (rows == jnp.broadcast_to(home[...], (16, PL))).astype(F32)
     smooth_matrix = s_ref[...]
     smat[0:CF, :], smat[CF : 2 * CF, :] = halves(smooth_matrix)
     whole = jnp.concatenate([blocks[k] for k in range(NB)], axis=1)
@@ -186,6 +204,29 @@
     pair_matrix(csmat, 0, CC, jnp.transpose(coarse_smooth, (1, 0)))
 
 
+def fetch(pairs, sems):
+    copies = [pltpu.make_async_copy(source, target, sems.at[n]) for n, (source, target) in enumerate(pairs)]
+    for copy in copies:
+        copy.start()
+    return copies
+
+
+def pack_kernel(rhs_far, weights_far, low, high, a0, a1, a2, a3, by_site, rhs, weights, sems):
+    for copy in fetch(((weights_far, weights), (rhs_far, rhs)), sems):
+        copy.wait()
+    for t, row in enumerate((a0, a1, a2, a3)):
+        for z in range(4):
+            field = rhs[pl.ds(4 * t + z, CF, stride=16), :]
+            links = weights[pl.ds(4 * t + z, 8, stride=16), :]
+            half, number = (high if z >= 2 else low), 2 * t + z % 2
+            half[number, 0:CF, :] = field
+            half[number, CF : CF + 8, :] = links
+            by_site[4 * t + z] = links
+            row[z, 0:CF, :] = field
+            if t in (0, 3):
+                row[z, CF : CF + 8, :] = links
+
+
 def local_kernel(
     a0, a1, a2, a3, l_ref, hzm, hzp, smat, mmat, plane_ref,
     x0, lw, x1,
@@ -196,9 +237,8 @@
         for pair in range(2):
             site = place(t, 2 * pair)
             slot = pair
-            smooth(smat, vhigh.at[slot], vlow.at[slot], x0, [row[2 * pair], row[2 * pair + 1]], [site, site + 1])
-        for z in range(4):
-            lw[place(t, z)] = l_ref[:, 4 * t + z, :]
+            smooth(smat, vhigh.at[slot], vlow.at[slot], x0, [row[2 * pair, 0:CF, :], row[2 * pair + 1, 0:CF, :]], [site, site + 1])
+        lw[pl.ds(place(t, 0), 4)] = l_ref[4 * t : 4 * t + 4]
         for slot, (source, z) in enumerate(((hzm, -2), (hzp, 4))):
             site = place(t, z)
             smooth(
@@ -253,7 +293,7 @@
 
     def finish(t, half, images):
         for column, image in enumerate(images):
-            restrict(4 * t + 2 * half + column, rows[t][2 * half + column] - image)
+            restrict(4 * t + 2 * half + column, rows[t][2 * half + column, 0:CF, :] - image)
 
     block_pairs(range(4), bmat, x1, lw, plane, vhigh, vlow, finish)
     for base, t, outside, hop in ((16, 3, 4, 1), (20, 0, -1, 0)):
@@ -460,7 +500,7 @@
     def finish(t, half, images):
         for column, image in enumerate(images):
             number = 4 * t + 2 * half + column
-            rest[number] = rows[t][2 * half + column] - image
+            rest[number] = rows[t][2 * half + column, 0:CF, :] - image
             copies.append(send(rest.at[number], res_out, number, 1))
 
     block_pairs(range(4), bmat, x4, lw, plane, vhigh, vlow, finish)
@@ -468,26 +508,31 @@
         copy.wait()
 
 
-STACKED = ((2, KF, 2 * PL), BF16)
+STACKED = ((2, 2, KF, PL), BF16)
 FRAME = ((64, CF, PL), F32)
 WEIGHTS = ((64, 8, PL), F32)
 ROW = ((4, CF, PL), F32)
 PAIRED = ((2 * CF, KF), BF16)
 
 
-def call(kernel, outs, scratch, aliases, *args, limit=8, far=()):
-    vmem, away = pl.BlockSpec(memory_space=pltpu.VMEM), pl.BlockSpec(memory_space=pl.ANY)
-    return pl.pallas_call(
+def call(kernel, outs, scratch, aliases, *args, limit=8, far=(), away=()):
+    vmem, hbm = pl.BlockSpec(memory_space=pltpu.VMEM), pl.BlockSpec(memory_space=pltpu.HBM)
+    built = pl.pallas_call(
         kernel,
         out_shape=tuple(jax.ShapeDtypeStruct(shape, kind) for shape, kind in outs),
-        in_specs=[vmem] * len(args),
-        out_specs=tuple(away if number in far else vmem for number in range(len(outs))),
+        in_specs=[hbm if number in away else vmem for number in range(len(args))],
+        out_specs=tuple(hbm if number in far else vmem for number in range(len(outs))),
         scratch_shapes=[
             pltpu.VMEM(*entry) if isinstance(entry, tuple) else entry for entry in scratch
         ],
         input_output_aliases=aliases,
         compiler_params=pltpu.CompilerParams(vmem_limit_bytes=limit << 20),
-    )(*args)
+    )
+    args = [
+        pltpu.with_memory_space_constraint(value, pltpu.HBM) if number in away else value
+        for number, value in enumerate(args)
+    ]
+    return built(*args)
 
 
 def moved(value, axes, step):
@@ -510,27 +555,23 @@
     coarse_smoother,
     coarse_next,
 ):
-    rows = [jnp.transpose(rhs_field[0, :, t], (1, 0, 2)) for t in range(4)]
-    lows, highs = (
-        jnp.concatenate(
-            [
-                jnp.transpose(rhs_field[0, :, :, z : z + 2], (1, 2, 0, 3)),
-                jnp.transpose(link_weights[:, :, z : z + 2], (1, 2, 0, 3)),
-            ],
-            axis=2,
-        ).reshape(8, CF + 8, PL)
-        for z in (0, 2)
-    )
-    ends = [
-        jnp.concatenate([rows[t], jnp.transpose(link_weights[:, t], (1, 0, 2))], axis=1) for t in (0, 3)
-    ]
+    near = ((4, CF + 8, PL), F32)
+    sides = ((8, CF + 8, PL), F32)
+    lows, highs, *rows, links = call(
+        pack_kernel,
+        (sides, sides, near, ROW, ROW, near, ((16, 8, PL), F32)),
+        (((CF * 16, PL), F32), ((8 * 16, PL), F32), pltpu.SemaphoreType.DMA((2,))),
+        {},
+        rhs_field.reshape(CF * 16, PL), link_weights.reshape(8 * 16, PL),
+        away=(0, 1),
+    )
     hzm, hzp = moved(highs, "gz", 1), moved(lows, "gz", -1)
-    tm1, tp1 = moved(ends[1], TAXES, 1), moved(ends[0], TAXES, -1)
+    tm1, tp1 = moved(rows[3], TAXES, 1), moved(rows[0], TAXES, -1)
     ctm = moved(jnp.stack([hzm[7, 0:CF], hzp[6, 0:CF]]), TAXES, 1)
     ctp = moved(jnp.stack([hzm[1, 0:CF], hzp[0, 0:CF]]), TAXES, -1)
 
     hops = ((2, 2 * CF, CF), BF16)
-    smat, mpair, bpair, cpair, csmat, mhops, bhops = call(
+    smat, mpair, bpair, cpair, csmat, mhops, bhops, restrict, prolong, plane, home, member = call(
         prepare_kernel,
         (
             ((2 * CF, CF), BF16),
@@ -540,29 +581,40 @@
             ((2 * CC, 2 * CC), BF16),
             hops,
             hops,
+            ((CF, CC), F32),
+            ((CF, CC), F32),
+            ((4, PL), jnp.int32),
+            ((1, PL), jnp.int32),
+            ((16, PL), F32),
         ),
-        (),
+        (
+            ((CF, CF), F32),
+            ((NB, CF, CF), F32),
+            ((CC, CC), F32),
+            ((NB, CC, CC), F32),
+            pltpu.SemaphoreType.DMA((8,)),
+        ),
         {},
-        smoother, fine_blocks, coarse_smoother, coarse_blocks,
-    )
-    member = (jnp.arange(16, dtype=jnp.int32)[:, None] == aggregate[None, :]).astype(F32)
+        smoother, fine_blocks, coarse_smoother, coarse_blocks, restrict_map, prolong_map.T, plane_next,
+        aggregate.reshape(1, PL),
+        away=range(8),
+    )
     turn = jnp.broadcast_to(coarse_next[:, :, None], (4, CP, CC))
-    home = jnp.broadcast_to(aggregate[None, :], (8, PL))
 
     x0, lw, x1 = call(
         local_kernel,
         (FRAME, WEIGHTS, FRAME),
         (STACKED, STACKED),
         {},
-        *rows, link_weights.reshape(8, 16, PL), hzm, hzp, smat, mpair, plane_next,
-    )
-    (x1,) = call(edge_kernel, (FRAME,), (STACKED, STACKED), {2: 0}, x0, lw, x1, mpair, plane_next)
+        *rows, links, hzm, hzp, smat, mpair, plane,
+    )
+    (x1,) = call(edge_kernel, (FRAME,), (STACKED, STACKED), {2: 0}, x0, lw, x1, mpair, plane)
     x0, lw, x1, up, down, first, last = call(
         pre_kernel,
         (FRAME, WEIGHTS, FRAME, ((20, CP, CC), F32), ((20, CP, CC), F32), ROW, ROW),
         (STACKED, STACKED, ((24 * CP, CF), F32)),
         {15: 0, 16: 1, 17: 2},
-        *rows, tm1, tp1, ctm, ctp, smat, bpair, mhops, bhops, restrict_map, plane_next, member,
+        *rows, tm1, tp1, ctm, ctp, smat, bpair, mhops, bhops, restrict, plane, member,
         x0, lw, x1,
     )
 
@@ -588,7 +640,7 @@
             ((76 * CP, 2 * KC), BF16),
         ),
         {},
-        whole, e2m, e2p, zcm, zcp, csmat, cpair, turn, prolong_map.T,
+        whole, e2m, e2p, zcm, zcp, csmat, cpair, turn, prolong,
         limit=12,
     )
     field, wide, r0, r3 = call(
@@ -596,7 +648,7 @@
         (FRAME, FRAME, ROW, ROW),
         (STACKED, STACKED),
         {},
-        lifted, home, plane_next, x1, xm, xp, x0, lw, mpair,
+        lifted, home, plane, x1, xm, xp, x0, lw, mpair,
     )
     half = ((8, CF, PL), F32)
     wide, r1, r2, low, high = call(
@@ -604,7 +656,7 @@
         (FRAME, ROW, ROW, half, half),
         (STACKED, STACKED),
         {1: 0},
-        field, wide, r0, r3, plane_next, x0, lw, mpair,
+        field, wide, r0, r3, plane, x0, lw, mpair,
     )
     tm1, tp1 = moved(r3, TAXES, 1), moved(r0, TAXES, -1)
     tm2, tp2 = moved(r2, TAXES, 1), moved(r1, TAXES, -1)
@@ -616,14 +668,14 @@
         (FRAME, FRAME),
         (STACKED, STACKED),
         {0: 0},
-        wide, hzm, hzp, x0, lw, mpair, plane_next,
+        wide, hzm, hzp, x0, lw, mpair, plane,
     )
     _, _, sol, res = call(
         post_kernel,
         (FRAME, FRAME, ((CF, 16, PL), F32), ((CF, 16, PL), F32)),
         (STACKED, STACKED, ((16, CF, PL), F32), pltpu.SemaphoreType.DMA((2, 16))),
         {0: 0, 1: 1},
-        wide, x4, tm1, tm2, tp1, tp2, czm, czp, *rows, x0, lw, mpair, bpair, mhops, plane_next,
+        wide, x4, tm1, tm2, tp1, tp2, czm, czp, *rows, x0, lw, mpair, bpair, mhops, plane,
         far=(2, 3),
     )
 

time: 101 us -> 92.8 us (0.919)
  the two profiles are of different devices: /device:TPU:0 before, /device:TPU:15 now
where the time goes in v1:
time: 92.8 us; the launch traced here: 92.6 us
  starting transfers between devices  42 us (45%)
  Pallas kernels  33.1 us (36%)
  waiting for transfers between devices  16.4 us (18%)
  between operations  1.01 us (1%)
    ppermute x22, starting transfers between devices, moved(): lax.ppermute(value, axes, [(i, (i + step) % count) for i in range(count)])  42 us
    pallas_call x11, Pallas kernels, call(): return built(*args)  33.1 us
    ppermute x22, waiting for transfers between devices, moved(): lax.ppermute(value, axes, [(i, (i + step) % count) for i in range(count)])  16.4 us
  transfers between devices with their start and end apart: 22, of which 6 were waited for; matrix products, arithmetic and copies ran while one was open for 0% of the time, Pallas kernels for 18%

profile of v1, /device:TPU:15, one launch (start us, length us, event | category | flops | bytes accessed | tf_op | source)
XLA Modules:
  0.0 92.6 jit_solution(10007086651798032218)
XLA Ops:
  0.6 1.5 %shard_map.122 = (f32[8,104,128]{2,1,0:T(8,128)S(1)}, f32[8,104,128]{2,1,0:T(8,128)S(1)}, f32[4,104,128]{2,1,0:T(8,128)S(1)}, f32[4,96,128]{2,1,0:T(8,128)S(1)},...) custom-call(f32[1536,128]{1,0:T(8,128)} %bitcast.6, f32[128,128]{1,0:T(8,128)} %bitcast.7), custom_call_target="tpu_custom_call" | custom-call | tf_op jit(solution)/shard_map/pallas_call | solution.py:535
  2.1 2.2 %collective-permute-start.2 = (f32[8,104,128]{2,1,0:T(8,128)S(1)}, f32[8,104,128]{2,1,0:T(8,128)S(1)}, u32[]{:S(2)}, u32[]{:S(2)}) collective-permute-start(f32[8,104,128]{2,1,0:T(8,128)S(1)} %get-tuple-element.50), channel_id=1, source_target_pairs={{0,2},{2,4},{4,6},{6,8},{8,10},{10,12},{12,14},{14,0},{1,3},{3,5},... | collective-permute-start | bytes 1277960 | tf_op jit(solution)/shard_map/ppermute | solution.py:542
  4.3 0.0 collective-permute-start.3
  4.3 2.3 %collective-permute-start.1 = (f32[4,104,128]{2,1,0:T(8,128)S(1)}, f32[4,104,128]{2,1,0:T(8,128)S(1)}, u32[]{:S(2)}, u32[]{:S(2)}) collective-permute-start(f32[4,104,128]{2,1,0:T(8,128)S(1)} %get-tuple-element.46.a0), channel_id=1, source_target_pairs={{0,113},{1,0},{16,1},{17,16},{32,17},{33,32},{48,33},{49,48},{64,4... | collective-permute-start | bytes 638984 | tf_op jit(solution)/shard_map/ppermute | solution.py:542
  6.6 0.7 collective-permute-start
  7.3 2.1 %collective-permute-done.2.hzm = f32[8,104,128]{2,1,0:T(8,128)S(1)} collective-permute-done((f32[8,104,128]{2,1,0:T(8,128)S(1)}, f32[8,104,128]{2,1,0:T(8,128)S(1)}, u32[]{:S(2)}, u32[]{:S(2)}) %collective-permute-start.2) | collective-permute-done | bytes 426016 | tf_op jit(solution)/shard_map/ppermute | solution.py:542
  9.4 2.8 %collective-permute-done.3.hzp = f32[8,104,128]{2,1,0:T(8,128)S(1)} collective-permute-done((f32[8,104,128]{2,1,0:T(8,128)S(1)}, f32[8,104,128]{2,1,0:T(8,128)S(1)}, u32[]{:S(2)}, u32[]{:S(2)}) %collective-permute-start.3) | collective-permute-done | bytes 426016 | tf_op jit(solution)/shard_map/ppermute | solution.py:542
  12.2 1.8 %collective-permute-start.4 = (f32[2,96,128]{2,1,0:T(8,128)S(1)}, f32[2,96,128]{2,1,0:T(8,128)S(1)}, u32[]{:S(2)}, u32[]{:S(2)}) collective-permute-start(f32[2,96,128]{2,1,0:T(8,128)S(1)} %pad_maximum_fusion), channel_id=1, source_target_pairs={{0,1},{1,16},{16,17},{17,32},{32,33},{33,48},{48,49},{49,64},{64,6... | collective-permute-start | bytes 294920 | tf_op jit(solution)/shard_map/ppermute | solution.py:542
  14.0 2.2 %collective-permute-start.5 = (f32[2,96,128]{2,1,0:T(8,128)S(1)}, f32[2,96,128]{2,1,0:T(8,128)S(1)}, u32[]{:S(2)}, u32[]{:S(2)}) collective-permute-start(f32[2,96,128]{2,1,0:T(8,128)S(1)} %pad_maximum_fusion.1), channel_id=1, source_target_pairs={{0,113},{1,0},{16,1},{17,16},{32,17},{33,32},{48,33},{49,48},{64,4... | collective-permute-start | bytes 294920 | tf_op jit(solution)/shard_map/ppermute | solution.py:542
  16.2 2.5 %shard_map.123 = (bf16[192,96]{1,0:T(8,128)(2,1)S(1)}, bf16[192,864]{1,0:T(8,128)(2,1)S(1)}, bf16[192,864]{1,0:T(8,128)(2,1)S(1)}, bf16[2304,256]{1,0:T(8,128)(2...) custom-call(f32[96,96]{1,0:T(8,128)} %s_far.1, ...), custom_call_target="tpu_custom_call" | custom-call | tf_op jit(solution)/shard_map/pallas_call | solution.py:535
  18.7 2.7 %shard_map.124 = (f32[64,96,128]{2,1,0:T(8,128)S(1)}, f32[64,8,128]{2,1,0:T(8,128)S(1)}, f32[64,96,128]{2,1,0:T(8,128)S(1)}) custom-call(f32[4,104,128]{2,1,0:T(8,128)S(1)} %get-tuple-element.46.a0, f32[4,96,128]{2,1,0:T(8,128)S(1)} %get-tuple-element.47.a1, f32[4,96,128]{2,1,0:T(8,128)S(1)} %get-tuple-element.48.a2, ...), custom_call_target="tpu_custom_call" | custom-call | tf_op jit(solution)/shard_map/pallas_call | solution.py:535
  21.4 2.0 %shard_map.125.x1_in = f32[64,96,128]{2,1,0:T(8,128)S(1)} custom-call(f32[64,96,128]{2,1,0:T(8,128)S(1)} %get-tuple-element.61.x0.x0_in, f32[64,8,128]{2,1,0:T(8,128)S(1)} %get-tuple-element.62.lw.lw_in, f32[64,96,128]{2,1,0:T(8,128)S(1)} %get-tuple-element.63.x1_in, bf16[192,864]{1,0:T(8,128)(2,1)S(1)} %get-tuple-element.60.mmat, ...), custom_call_target="tpu_custom_call", output_to_operand_aliasing={{}: (2, {})} | custom-call | tf_op jit(solution)/shard_map/pallas_call | solution.py:535
  23.5 0.0 collective-permute-done.1.tp1
  23.5 0.0 collective-permute-done.4.ctm
  23.5 0.0 collective-permute-done.5.ctp
  23.5 0.0 copy-start
  23.5 6.7 %shard_map.126 = (f32[64,96,128]{2,1,0:T(8,128)S(1)}, f32[64,8,128]{2,1,0:T(8,128)S(1)}, f32[64,96,128]{2,1,0:T(8,128)S(1)}, f32[20,8,128]{2,1,0:T(8,128)S(1)}, ...) custom-call(f32[4,104,128]{2,1,0:T(8,128)S(1)} %get-tuple-element.46, ...), custom_call_target="tpu_custom_call", output_to_operand_aliasing={{0}: (15, {}), {1}: (16, {}), {2}: (17, {})} | custom-call | tf_op jit(solution)/shard_map/pallas_call | solution.py:535
  30.3 0.9 collective-permute-start.6
  31.1 3.0 %collective-permute-start.7 = (f32[20,8,128]{2,1,0:T(8,128)S(1)}, f32[20,8,128]{2,1,0:T(8,128)S(1)}, u32[]{:S(2)}, u32[]{:S(2)}) collective-permute-start(f32[20,8,128]{2,1,0:T(8,128)S(1)} %get-tuple-element.65.down), channel_id=1, source_target_pairs={{0,113},{1,0},{16,1},{17,16},{32,17},{33,32},{48,33},{49,48},{64,4... | collective-permute-start | bytes 245768 | tf_op jit(solution)/shard_map/ppermute | solution.py:542
  34.2 0.0 collective-permute-start.12
  34.2 3.9 %collective-permute-start.13 = (f32[4,96,128]{2,1,0:T(8,128)S(1)}, f32[4,96,128]{2,1,0:T(8,128)S(1)}, u32[]{:S(2)}, u32[]{:S(2)}) collective-permute-start(f32[4,96,128]{2,1,0:T(8,128)S(1)} %get-tuple-element.74), channel_id=1, source_target_pairs={{0,113},{1,0},{16,1},{17,16},{32,17},{33,32},{48,33},{49,48},{64,4... | collective-permute-start | bytes 589832 | tf_op jit(solution)/shard_map/ppermute | solution.py:542
  38.1 0.0 collective-permute-done.6.tcm
  38.1 0.6 collective-permute-done.7.tcp
  38.7 1.0 %collective-permute-start.11 = (f32[40,8,128]{2,1,0:T(8,128)S(1)}, f32[40,8,128]{2,1,0:T(8,128)S(1)}, u32[]{:S(2)}, u32[]{:S(2)}) collective-permute-start(f32[40,8,128]{2,1,0:T(8,128)S(1)} %get-tuple-element.67), channel_id=1, source_target_pairs={{0,14},{2,0},{4,2},{6,4},{8,6},{10,8},{12,10},{14,12},{1,15},{3,1}... | collective-permute-start | bytes 491528 | tf_op jit(solution)/shard_map/ppermute | solution.py:542
  39.7 0.7 collective-permute-start.10
  40.5 0.7 collective-permute-start.9
  41.2 4.2 %collective-permute-done.9.e2p = f32[4,8,128]{2,1,0:T(8,128)S(1)} collective-permute-done((f32[4,8,128]{2,1,0:T(8,128)S(1)}, f32[4,8,128]{2,1,0:T(8,128)S(1)}, u32[]{:S(2)}, u32[]{:S(2)}) %collective-permute-start.9) | collective-permute-done | bytes 16416 | tf_op jit(solution)/shard_map/ppermute | solution.py:542
  45.4 1.2 %collective-permute-start.8 = (f32[4,8,128]{2,1,0:T(8,128)S(1)}, f32[4,8,128]{2,1,0:T(8,128)S(1)}, u32[]{:S(2)}, u32[]{:S(2)}) collective-permute-start(f32[4,8,128]{2,1,0:T(8,128)S(1)} %slice.34), channel_id=1, source_target_pairs={{0,16},{1,17},{16,32},{17,33},{32,48},{33,49},{48,64},{49,65},{64,... | collective-permute-start | bytes 49160 | tf_op jit(solution)/shard_map/ppermute | solution.py:542
  46.5 1.4 %collective-permute-done.8.e2m = f32[4,8,128]{2,1,0:T(8,128)S(1)} collective-permute-done((f32[4,8,128]{2,1,0:T(8,128)S(1)}, f32[4,8,128]{2,1,0:T(8,128)S(1)}, u32[]{:S(2)}, u32[]{:S(2)}) %collective-permute-start.8) | collective-permute-done | bytes 16416 | tf_op jit(solution)/shard_map/ppermute | solution.py:542
  47.9 0.0 collective-permute-done.11.zcp
  47.9 0.0 collective-permute-done.10.zcm
  48.0 0.1 broadcast_in_dim.2.coarse_ref
  48.0 4.0 %shard_map.128.lifted = f32[3,96,128]{2,1,0:T(8,128)S(1)} custom-call(f32[48,8,128]{2,1,0:T(8,128)S(1)} %get-tuple-element.66.whole, f32[4,8,128]{2,1,0:T(8,128)S(1)} %collective-permute-done.8.e2m, f32[4,8,128]{2,1,0:T(8,128)S(1)} %collective-permute-done.9.e2p, f32[40,8,128]{2,1,0:T(8,128)S(1)} %collective-permute-done.10.zcm, ...), custom_call_target="tpu_custom_call" | custom-call | tf_op jit(solution)/shard_map/pallas_call | solution.py:535
  52.1 0.0 collective-permute-done.12.xm
  52.1 3.0 %shard_map.129 = (f32[64,96,128]{2,1,0:T(8,128)S(1)}, f32[64,96,128]{2,1,0:T(8,128)S(1)}, f32[4,96,128]{2,1,0:T(8,128)S(1)}, f32[4,96,128]{2,1,0:T(8,128)S(1)}) custom-call(f32[3,96,128]{2,1,0:T(8,128)S(1)} %shard_map.128.lifted, s32[1,128]{1,0:T(1,128)S(1)} %get-tuple-element.71.lift_ref, s32[4,128]{1,0:T(4,128)S(1)} %get-tuple-element.57.plane_ref, ...), custom_call_target="tpu_custom_call" | custom-call | tf_op jit(solution)/shard_map/pallas_call | solution.py:535
  55.1 3.3 %collective-permute-start.18 = (f32[4,96,128]{2,1,0:T(8,128)S(1)}, f32[4,96,128]{2,1,0:T(8,128)S(1)}, u32[]{:S(2)}, u32[]{:S(2)}) collective-permute-start(f32[4,96,128]{2,1,0:T(8,128)S(1)} %get-tuple-element.79.first), channel_id=1, source_target_pairs={{0,113},{1,0},{16,1},{17,16},{32,17},{33,32},{48,33},{49,48},{64,4... | collective-permute-start | bytes 589832 | tf_op jit(solution)/shard_map/ppermute | solution.py:542
  58.5 0.6 collective-permute-start.16
  59.1 1.4 %shard_map.130 = (f32[64,96,128]{2,1,0:T(8,128)S(1)}, f32[4,96,128]{2,1,0:T(8,128)S(1)}, f32[4,96,128]{2,1,0:T(8,128)S(1)}, f32[8,96,128]{2,1,0:T(8,128)S(1)}, f32[8,96,128]{2,1,0:T(8,128)S(1)}) custom-call(f32[64,96,128]{2,1,0:T(8,128)S(1)} %get-tuple-element.77.field, ...), custom_call_target="tpu_custom_call", output_to_operand_aliasing={{0}: (1, {})} | custom-call | tf_op jit(solution)/shard_map/pallas_call | solution.py:535
  60.5 4.8 %collective-permute-start.17 = (f32[4,96,128]{2,1,0:T(8,128)S(1)}, f32[4,96,128]{2,1,0:T(8,128)S(1)}, u32[]{:S(2)}, u32[]{:S(2)}) collective-permute-start(f32[4,96,128]{2,1,0:T(8,128)S(1)} %get-tuple-element.86), channel_id=1, source_target_pairs={{0,1},{1,16},{16,17},{17,32},{32,33},{33,48},{48,49},{49,64},{64,6... | collective-permute-start | bytes 589832 | tf_op jit(solution)/shard_map/ppermute | solution.py:542
  65.2 0.0 collective-permute-start.19
  65.2 4.4 %collective-permute-start.14 = (f32[8,96,128]{2,1,0:T(8,128)S(1)}, f32[8,96,128]{2,1,0:T(8,128)S(1)}, u32[]{:S(2)}, u32[]{:S(2)}) collective-permute-start(f32[8,96,128]{2,1,0:T(8,128)S(1)} %get-tuple-element.82), channel_id=1, source_target_pairs={{0,2},{2,4},{4,6},{6,8},{8,10},{10,12},{12,14},{14,0},{1,3},{3,5},... | collective-permute-start | bytes 1179656 | tf_op jit(solution)/shard_map/ppermute | solution.py:542
  69.7 0.0 collective-permute-done.18.tp1
  69.7 6.7 %collective-permute-start.15 = (f32[8,96,128]{2,1,0:T(8,128)S(1)}, f32[8,96,128]{2,1,0:T(8,128)S(1)}, u32[]{:S(2)}, u32[]{:S(2)}) collective-permute-start(f32[8,96,128]{2,1,0:T(8,128)S(1)} %get-tuple-element.83), channel_id=1, source_target_pairs={{0,14},{2,0},{4,2},{6,4},{8,6},{10,8},{12,10},{14,12},{1,15},{3,1}... | collective-permute-start | bytes 1179656 | tf_op jit(solution)/shard_map/ppermute | solution.py:542
  76.4 1.5 %collective-permute-start.20 = (f32[2,96,128]{2,1,0:T(8,128)S(1)}, f32[2,96,128]{2,1,0:T(8,128)S(1)}, u32[]{:S(2)}, u32[]{:S(2)}) collective-permute-start(f32[2,96,128]{2,1,0:T(8,128)S(1)} %pad_maximum_fusion.2), channel_id=1, source_target_pairs={{0,2},{2,4},{4,6},{6,8},{8,10},{10,12},{12,14},{14,0},{1,3},{3,5},... | collective-permute-start | bytes 294920 | tf_op jit(solution)/shard_map/ppermute | solution.py:542
  77.9 0.0 collective-permute-start.21
  77.9 5.3 %collective-permute-done.15.hzp = f32[8,96,128]{2,1,0:T(8,128)S(1)} collective-permute-done((f32[8,96,128]{2,1,0:T(8,128)S(1)}, f32[8,96,128]{2,1,0:T(8,128)S(1)}, u32[]{:S(2)}, u32[]{:S(2)}) %collective-permute-start.15) | collective-permute-done | bytes 393248 | tf_op jit(solution)/shard_map/ppermute | solution.py:542
  83.3 4.0 %shard_map.131 = (f32[64,96,128]{2,1,0:T(8,128)S(1)}, f32[64,96,128]{2,1,0:T(8,128)S(1)}) custom-call(f32[64,96,128]{2,1,0:T(8,128)S(1)} %get-tuple-element.81.wide_in, f32[8,96,128]{2,1,0:T(8,128)S(1)} %collective-permute-done.14.hzm, f32[8,96,128]{2,1,0:T(8,128)S(1)} %collective-permute-done.15.hzp, ...), custom_call_target="tpu_custom_call", output_to_operand_aliasing={{0}: (0, {})} | custom-call | tf_op jit(solution)/shard_map/pallas_call | solution.py:535
  87.3 5.2 %shard_map.132 = (f32[64,96,128]{2,1,0:T(8,128)S(1)}, f32[64,96,128]{2,1,0:T(8,128)S(1)}, f32[96,16,128]{2,1,0:T(8,128)}, f32[96,16,128]{2,1,0:T(8,128)}) custom-call(f32[64,96,128]{2,1,0:T(8,128)S(1)} %get-tuple-element.84.wide_in, f32[64,96,128]{2,1,0:T(8,128)S(1)} %get-tuple-element.85.x4_in, ...), custom_call_target="tpu_custom_call", output_to_operand_aliasing={{0}: (0, {}), {1}: (1, {})} | custom-call | tf_op jit(solution)/shard_map/pallas_call | solution.py:535
  (20 shorter events, 0.1 us)
Async XLA Ops:
  2.1 7.3 %collective-permute-start.2 = (f32[8,104,128]{2,1,0:T(8,128)S(1)}, f32[8,104,128]{2,1,0:T(8,128)S(1)}, u32[]{:S(2)}, u32[]{:S(2)}) collective-permute-start(f32[8,104,128]{2,1,0:T(8,128)S(1)} %get-tuple-element.50), channel_id=1, source_target_pairs={{0,2},{2,4},{4,6},{6,8},{8,10},{10,12},{12,14},{14,0},{1,3},{3,5},... | collective-permute-start | bytes 1277960 | tf_op jit(solution)/shard_map/ppermute | solution.py:542
  4.3 7.8 %collective-permute-start.3 = (f32[8,104,128]{2,1,0:T(8,128)S(1)}, f32[8,104,128]{2,1,0:T(8,128)S(1)}, u32[]{:S(2)}, u32[]{:S(2)}) collective-permute-start(f32[8,104,128]{2,1,0:T(8,128)S(1)} %get-tuple-element.51), channel_id=1, source_target_pairs={{0,14},{2,0},{4,2},{6,4},{8,6},{10,8},{12,10},{14,12},{1,15},{3,1}... | collective-permute-start | bytes 1277960 | tf_op jit(solution)/shard_map/ppermute | solution.py:542
  4.3 19.1 %collective-permute-start.1 = (f32[4,104,128]{2,1,0:T(8,128)S(1)}, f32[4,104,128]{2,1,0:T(8,128)S(1)}, u32[]{:S(2)}, u32[]{:S(2)}) collective-permute-start(f32[4,104,128]{2,1,0:T(8,128)S(1)} %get-tuple-element.46.a0), channel_id=1, source_target_pairs={{0,113},{1,0},{16,1},{17,16},{32,17},{33,32},{48,33},{49,48},{64,4... | collective-permute-start | bytes 638984 | tf_op jit(solution)/shard_map/ppermute | solution.py:542
  6.6 16.9 %collective-permute-start = (f32[4,104,128]{2,1,0:T(8,128)S(1)}, f32[4,104,128]{2,1,0:T(8,128)S(1)}, u32[]{:S(2)}, u32[]{:S(2)}) collective-permute-start(f32[4,104,128]{2,1,0:T(8,128)S(1)} %get-tuple-element.49.a3), channel_id=1, source_target_pairs={{0,1},{1,16},{16,17},{17,32},{32,33},{33,48},{48,49},{49,64},{64,6... | collective-permute-start | bytes 638984 | tf_op jit(solution)/shard_map/ppermute | solution.py:542
  12.2 11.3 %collective-permute-start.4 = (f32[2,96,128]{2,1,0:T(8,128)S(1)}, f32[2,96,128]{2,1,0:T(8,128)S(1)}, u32[]{:S(2)}, u32[]{:S(2)}) collective-permute-start(f32[2,96,128]{2,1,0:T(8,128)S(1)} %pad_maximum_fusion), channel_id=1, source_target_pairs={{0,1},{1,16},{16,17},{17,32},{32,33},{33,48},{48,49},{49,64},{64,6... | collective-permute-start | bytes 294920 | tf_op jit(solution)/shard_map/ppermute | solution.py:542
  14.0 9.5 %collective-permute-start.5 = (f32[2,96,128]{2,1,0:T(8,128)S(1)}, f32[2,96,128]{2,1,0:T(8,128)S(1)}, u32[]{:S(2)}, u32[]{:S(2)}) collective-permute-start(f32[2,96,128]{2,1,0:T(8,128)S(1)} %pad_maximum_fusion.1), channel_id=1, source_target_pairs={{0,113},{1,0},{16,1},{17,16},{32,17},{33,32},{48,33},{49,48},{64,4... | collective-permute-start | bytes 294920 | tf_op jit(solution)/shard_map/ppermute | solution.py:542
  23.5 24.5 %copy-start = (s32[4,8]{1,0:T(4,128)S(1)}, s32[4,8]{1,0:T(4,128)}, u32[]{:S(2)}) copy-start(s32[4,8]{1,0:T(4,128)} %param.21) | copy-start | bytes 388
  30.3 7.8 %collective-permute-start.6 = (f32[20,8,128]{2,1,0:T(8,128)S(1)}, f32[20,8,128]{2,1,0:T(8,128)S(1)}, u32[]{:S(2)}, u32[]{:S(2)}) collective-permute-start(f32[20,8,128]{2,1,0:T(8,128)S(1)} %get-tuple-element.64.up), channel_id=1, source_target_pairs={{0,1},{1,16},{16,17},{17,32},{32,33},{33,48},{48,49},{49,64},{64,6... | collective-permute-start | bytes 245768 | tf_op jit(solution)/shard_map/ppermute | solution.py:542
  31.1 7.5 %collective-permute-start.7 = (f32[20,8,128]{2,1,0:T(8,128)S(1)}, f32[20,8,128]{2,1,0:T(8,128)S(1)}, u32[]{:S(2)}, u32[]{:S(2)}) collective-permute-start(f32[20,8,128]{2,1,0:T(8,128)S(1)} %get-tuple-element.65.down), channel_id=1, source_target_pairs={{0,113},{1,0},{16,1},{17,16},{32,17},{33,32},{48,33},{49,48},{64,4... | collective-permute-start | bytes 245768 | tf_op jit(solution)/shard_map/ppermute | solution.py:542
  34.2 17.9 %collective-permute-start.12 = (f32[4,96,128]{2,1,0:T(8,128)S(1)}, f32[4,96,128]{2,1,0:T(8,128)S(1)}, u32[]{:S(2)}, u32[]{:S(2)}) collective-permute-start(f32[4,96,128]{2,1,0:T(8,128)S(1)} %get-tuple-element.73), channel_id=1, source_target_pairs={{0,1},{1,16},{16,17},{17,32},{32,33},{33,48},{48,49},{49,64},{64,6... | collective-permute-start | bytes 589832 | tf_op jit(solution)/shard_map/ppermute | solution.py:542
  34.2 17.9 %collective-permute-start.13 = (f32[4,96,128]{2,1,0:T(8,128)S(1)}, f32[4,96,128]{2,1,0:T(8,128)S(1)}, u32[]{:S(2)}, u32[]{:S(2)}) collective-permute-start(f32[4,96,128]{2,1,0:T(8,128)S(1)} %get-tuple-element.74), channel_id=1, source_target_pairs={{0,113},{1,0},{16,1},{17,16},{32,17},{33,32},{48,33},{49,48},{64,4... | collective-permute-start | bytes 589832 | tf_op jit(solution)/shard_map/ppermute | solution.py:542
  38.7 9.2 %collective-permute-start.11 = (f32[40,8,128]{2,1,0:T(8,128)S(1)}, f32[40,8,128]{2,1,0:T(8,128)S(1)}, u32[]{:S(2)}, u32[]{:S(2)}) collective-permute-start(f32[40,8,128]{2,1,0:T(8,128)S(1)} %get-tuple-element.67), channel_id=1, source_target_pairs={{0,14},{2,0},{4,2},{6,4},{8,6},{10,8},{12,10},{14,12},{1,15},{3,1}... | collective-permute-start | bytes 491528 | tf_op jit(solution)/shard_map/ppermute | solution.py:542
  39.7 8.2 %collective-permute-start.10 = (f32[40,8,128]{2,1,0:T(8,128)S(1)}, f32[40,8,128]{2,1,0:T(8,128)S(1)}, u32[]{:S(2)}, u32[]{:S(2)}) collective-permute-start(f32[40,8,128]{2,1,0:T(8,128)S(1)} %get-tuple-element.67), channel_id=1, source_target_pairs={{0,2},{2,4},{4,6},{6,8},{8,10},{10,12},{12,14},{14,0},{1,3},{3,5},... | collective-permute-start | bytes 491528 | tf_op jit(solution)/shard_map/ppermute | solution.py:542
  40.5 4.9 %collective-permute-start.9 = (f32[4,8,128]{2,1,0:T(8,128)S(1)}, f32[4,8,128]{2,1,0:T(8,128)S(1)}, u32[]{:S(2)}, u32[]{:S(2)}) collective-permute-start(f32[4,8,128]{2,1,0:T(8,128)S(1)} %slice.35), channel_id=1, source_target_pairs={{0,112},{1,113},{16,0},{17,1},{32,16},{33,17},{48,32},{49,33},{64,... | collective-permute-start | bytes 49160 | tf_op jit(solution)/shard_map/ppermute | solution.py:542
  45.4 2.6 %collective-permute-start.8 = (f32[4,8,128]{2,1,0:T(8,128)S(1)}, f32[4,8,128]{2,1,0:T(8,128)S(1)}, u32[]{:S(2)}, u32[]{:S(2)}) collective-permute-start(f32[4,8,128]{2,1,0:T(8,128)S(1)} %slice.34), channel_id=1, source_target_pairs={{0,16},{1,17},{16,32},{17,33},{32,48},{33,49},{48,64},{49,65},{64,... | collective-permute-start | bytes 49160 | tf_op jit(solution)/shard_map/ppermute | solution.py:542
  55.1 14.5 %collective-permute-start.18 = (f32[4,96,128]{2,1,0:T(8,128)S(1)}, f32[4,96,128]{2,1,0:T(8,128)S(1)}, u32[]{:S(2)}, u32[]{:S(2)}) collective-permute-start(f32[4,96,128]{2,1,0:T(8,128)S(1)} %get-tuple-element.79.first), channel_id=1, source_target_pairs={{0,113},{1,0},{16,1},{17,16},{32,17},{33,32},{48,33},{49,48},{64,4... | collective-permute-start | bytes 589832 | tf_op jit(solution)/shard_map/ppermute | solution.py:542
  58.5 17.9 %collective-permute-start.16 = (f32[4,96,128]{2,1,0:T(8,128)S(1)}, f32[4,96,128]{2,1,0:T(8,128)S(1)}, u32[]{:S(2)}, u32[]{:S(2)}) collective-permute-start(f32[4,96,128]{2,1,0:T(8,128)S(1)} %get-tuple-element.80.last), channel_id=1, source_target_pairs={{0,1},{1,16},{16,17},{17,32},{32,33},{33,48},{48,49},{49,64},{64,6... | collective-permute-start | bytes 589832 | tf_op jit(solution)/shard_map/ppermute | solution.py:542
  60.5 26.8 %collective-permute-start.17 = (f32[4,96,128]{2,1,0:T(8,128)S(1)}, f32[4,96,128]{2,1,0:T(8,128)S(1)}, u32[]{:S(2)}, u32[]{:S(2)}) collective-permute-start(f32[4,96,128]{2,1,0:T(8,128)S(1)} %get-tuple-element.86), channel_id=1, source_target_pairs={{0,1},{1,16},{16,17},{17,32},{32,33},{33,48},{48,49},{49,64},{64,6... | collective-permute-start | bytes 589832 | tf_op jit(solution)/shard_map/ppermute | solution.py:542
  65.2 22.0 %collective-permute-start.19 = (f32[4,96,128]{2,1,0:T(8,128)S(1)}, f32[4,96,128]{2,1,0:T(8,128)S(1)}, u32[]{:S(2)}, u32[]{:S(2)}) collective-permute-start(f32[4,96,128]{2,1,0:T(8,128)S(1)} %get-tuple-element.87), channel_id=1, source_target_pairs={{0,113},{1,0},{16,1},{17,16},{32,17},{33,32},{48,33},{49,48},{64,4... | collective-permute-start | bytes 589832 | tf_op jit(solution)/shard_map/ppermute | solution.py:542
  65.2 12.7 %collective-permute-start.14 = (f32[8,96,128]{2,1,0:T(8,128)S(1)}, f32[8,96,128]{2,1,0:T(8,128)S(1)}, u32[]{:S(2)}, u32[]{:S(2)}) collective-permute-start(f32[8,96,128]{2,1,0:T(8,128)S(1)} %get-tuple-element.82), channel_id=1, source_target_pairs={{0,2},{2,4},{4,6},{6,8},{8,10},{10,12},{12,14},{14,0},{1,3},{3,5},... | collective-permute-start | bytes 1179656 | tf_op jit(solution)/shard_map/ppermute | solution.py:542
  69.7 13.6 %collective-permute-start.15 = (f32[8,96,128]{2,1,0:T(8,128)S(1)}, f32[8,96,128]{2,1,0:T(8,128)S(1)}, u32[]{:S(2)}, u32[]{:S(2)}) collective-permute-start(f32[8,96,128]{2,1,0:T(8,128)S(1)} %get-tuple-element.83), channel_id=1, source_target_pairs={{0,14},{2,0},{4,2},{6,4},{8,6},{10,8},{12,10},{14,12},{1,15},{3,1}... | collective-permute-start | bytes 1179656 | tf_op jit(solution)/shard_map/ppermute | solution.py:542
  76.4 10.9 %collective-permute-start.20 = (f32[2,96,128]{2,1,0:T(8,128)S(1)}, f32[2,96,128]{2,1,0:T(8,128)S(1)}, u32[]{:S(2)}, u32[]{:S(2)}) collective-permute-start(f32[2,96,128]{2,1,0:T(8,128)S(1)} %pad_maximum_fusion.2), channel_id=1, source_target_pairs={{0,2},{2,4},{4,6},{6,8},{8,10},{10,12},{12,14},{14,0},{1,3},{3,5},... | collective-permute-start | bytes 294920 | tf_op jit(solution)/shard_map/ppermute | solution.py:542
  77.9 9.4 %collective-permute-start.21 = (f32[2,96,128]{2,1,0:T(8,128)S(1)}, f32[2,96,128]{2,1,0:T(8,128)S(1)}, u32[]{:S(2)}, u32[]{:S(2)}) collective-permute-start(f32[2,96,128]{2,1,0:T(8,128)S(1)} %pad_maximum_fusion.3), channel_id=1, source_target_pairs={{0,14},{2,0},{4,2},{6,4},{8,6},{10,8},{12,10},{14,12},{1,15},{3,1}... | collective-permute-start | bytes 294920 | tf_op jit(solution)/shard_map/ppermute | solution.py:542

commit v2 on v1

--- a/solution.py
+++ b/solution.py
@@ -173,20 +173,7 @@
     target[depth + row : depth + row + CC, CC : 2 * CC] = jnp.zeros((CC, CC), BF16)
 
 
-def prepare_kernel(
-    s_far, blocks_far, cs_far, coarse_far, r_far, prolong_far, plane_far, aggregate_far,
-    smat, mmat, bmat, cmat, csmat, mhops, bhops, restrict, prolong, plane, home, member,
-    s_ref, blocks, cs_ref, coarse, sems,
-):
-    copies = fetch(
-        (
-            (s_far, s_ref), (blocks_far, blocks), (cs_far, cs_ref), (coarse_far, coarse),
-            (r_far, restrict), (prolong_far, prolong), (plane_far, plane), (aggregate_far, home),
-        ),
-        sems,
-    )
-    for copy in copies:
-        copy.wait()
+def prepare_kernel(s_ref, blocks, home, smat, mmat, bmat, mhops, bhops, member):
     rows = lax.broadcasted_iota(jnp.int32, (16, PL), 0)
     member[...] = (rows == jnp.broadcast_to(home[...], (16, PL))).astype(F32)
     smooth_matrix = s_ref[...]
@@ -198,6 +185,12 @@
         block = blocks[hop + 1]
         bhops[hop, 0:CF, :], bhops[hop, CF : 2 * CF, :] = halves(block)
         mhops[hop, 0:CF, :], mhops[hop, CF : 2 * CF, :] = halves(exact_dot(smooth_matrix, block))
+
+
+def ready_kernel(cs_far, coarse_far, prolong_far, cmat, csmat, prolong, cs_ref, coarse, sems):
+    copies = fetch(((cs_far, cs_ref), (coarse_far, coarse), (prolong_far, prolong)), sems)
+    for copy in copies:
+        copy.wait()
     coarse_smooth = cs_ref[...]
     for k in range(NB):
         pair_matrix(cmat, k * CC, KC, jnp.transpose(exact_dot(coarse_smooth, coarse[k]), (1, 0)))
@@ -211,9 +204,20 @@
     return copies
 
 
-def pack_kernel(rhs_far, weights_far, low, high, a0, a1, a2, a3, by_site, rhs, weights, sems):
-    for copy in fetch(((weights_far, weights), (rhs_far, rhs)), sems):
-        copy.wait()
+def pack_kernel(
+    rhs_far, weights_far, s_far, blocks_far, r_far, plane_far, aggregate_far,
+    low, high, a0, a1, a2, a3, by_site, s_ref, blocks, restrict, plane, home,
+    rhs, weights, sems,
+):
+    copies = fetch(
+        (
+            (weights_far, weights), (rhs_far, rhs), (s_far, s_ref), (blocks_far, blocks),
+            (r_far, restrict), (plane_far, plane), (aggregate_far, home),
+        ),
+        sems,
+    )
+    copies[0].wait()
+    copies[1].wait()
     for t, row in enumerate((a0, a1, a2, a3)):
         for z in range(4):
             field = rhs[pl.ds(4 * t + z, CF, stride=16), :]
@@ -225,6 +229,8 @@
             row[z, 0:CF, :] = field
             if t in (0, 3):
                 row[z, CF : CF + 8, :] = links
+    for copy in copies[2:]:
+        copy.wait()
 
 
 def local_kernel(
@@ -557,13 +563,17 @@
 ):
     near = ((4, CF + 8, PL), F32)
     sides = ((8, CF + 8, PL), F32)
-    lows, highs, *rows, links = call(
+    lows, highs, *rows, links, s_near, blocks, restrict, plane, home = call(
         pack_kernel,
-        (sides, sides, near, ROW, ROW, near, ((16, 8, PL), F32)),
-        (((CF * 16, PL), F32), ((8 * 16, PL), F32), pltpu.SemaphoreType.DMA((2,))),
+        (
+            sides, sides, near, ROW, ROW, near, ((16, 8, PL), F32), ((CF, CF), F32), ((NB, CF, CF), F32),
+            ((CF, CC), F32), ((4, PL), jnp.int32), ((1, PL), jnp.int32),
+        ),
+        (((CF * 16, PL), F32), ((8 * 16, PL), F32), pltpu.SemaphoreType.DMA((7,))),
         {},
-        rhs_field.reshape(CF * 16, PL), link_weights.reshape(8 * 16, PL),
-        away=(0, 1),
+        rhs_field.reshape(CF * 16, PL), link_weights.reshape(8 * 16, PL), smoother, fine_blocks,
+        restrict_map, plane_next, aggregate.reshape(1, PL),
+        away=range(7),
     )
     hzm, hzp = moved(highs, "gz", 1), moved(lows, "gz", -1)
     tm1, tp1 = moved(rows[3], TAXES, 1), moved(rows[0], TAXES, -1)
@@ -571,33 +581,20 @@
     ctp = moved(jnp.stack([hzm[1, 0:CF], hzp[0, 0:CF]]), TAXES, -1)
 
     hops = ((2, 2 * CF, CF), BF16)
-    smat, mpair, bpair, cpair, csmat, mhops, bhops, restrict, prolong, plane, home, member = call(
+    smat, mpair, bpair, mhops, bhops, member = call(
         prepare_kernel,
-        (
-            ((2 * CF, CF), BF16),
-            PAIRED,
-            PAIRED,
-            ((2 * KC, 2 * CC), BF16),
-            ((2 * CC, 2 * CC), BF16),
-            hops,
-            hops,
-            ((CF, CC), F32),
-            ((CF, CC), F32),
-            ((4, PL), jnp.int32),
-            ((1, PL), jnp.int32),
-            ((16, PL), F32),
-        ),
-        (
-            ((CF, CF), F32),
-            ((NB, CF, CF), F32),
-            ((CC, CC), F32),
-            ((NB, CC, CC), F32),
-            pltpu.SemaphoreType.DMA((8,)),
-        ),
+        (((2 * CF, CF), BF16), PAIRED, PAIRED, hops, hops, ((16, PL), F32)),
+        (),
         {},
-        smoother, fine_blocks, coarse_smoother, coarse_blocks, restrict_map, prolong_map.T, plane_next,
-        aggregate.reshape(1, PL),
-        away=range(8),
+        s_near, blocks, home,
+    )
+    cpair, csmat, prolong = call(
+        ready_kernel,
+        (((2 * KC, 2 * CC), BF16), ((2 * CC, 2 * CC), BF16), ((CF, CC), F32)),
+        (((CC, CC), F32), ((NB, CC, CC), F32), pltpu.SemaphoreType.DMA((3,))),
+        {},
+        coarse_smoother, coarse_blocks, prolong_map.T,
+        away=range(3),
     )
     turn = jnp.broadcast_to(coarse_next[:, :, None], (4, CP, CC))
 

time: 92.8 us -> 94.3 us (1.016)
  the two profiles are of different devices: /device:TPU:15 before, /device:TPU:5 now
where the time goes in v2:
time: 94.3 us; the launch traced here: 94.1 us
  starting transfers between devices  41.8 us (44%)
  Pallas kernels  33.1 us (35%)
  waiting for transfers between devices  18 us (19%)
  between operations  1.07 us (1%)
    ppermute x22, starting transfers between devices, moved(): lax.ppermute(value, axes, [(i, (i + step) % count) for i in range(count)])  41.8 us
    pallas_call x12, Pallas kernels, call(): return built(*args)  33.1 us
    ppermute x22, waiting for transfers between devices, moved(): lax.ppermute(value, axes, [(i, (i + step) % count) for i in range(count)])  18 us
  transfers between devices with their start and end apart: 22, of which 6 were waited for; matrix products, arithmetic and copies ran while one was open for 0% of the time, Pallas kernels for 18%

profile of v2, /device:TPU:5, one launch (start us, length us, event | category | flops | bytes accessed | tf_op | source)
XLA Modules:
  0.0 94.1 jit_solution(9818649963755778564)
XLA Ops:
  0.6 1.5 %shard_map.122 = (f32[8,104,128]{2,1,0:T(8,128)S(1)}, f32[8,104,128]{2,1,0:T(8,128)S(1)}, f32[4,104,128]{2,1,0:T(8,128)S(1)}, f32[4,96,128]{2,1,0:T(8,128)S(1)},...) custom-call(f32[1536,128]{1,0:T(8,128)} %bitcast.6, ...), custom_call_target="tpu_custom_call" | custom-call | tf_op jit(solution)/shard_map/pallas_call | solution.py:541
  2.2 2.2 %collective-permute-start.2 = (f32[8,104,128]{2,1,0:T(8,128)S(1)}, f32[8,104,128]{2,1,0:T(8,128)S(1)}, u32[]{:S(2)}, u32[]{:S(2)}) collective-permute-start(f32[8,104,128]{2,1,0:T(8,128)S(1)} %get-tuple-element.52), channel_id=1, source_target_pairs={{0,2},{2,4},{4,6},{6,8},{8,10},{10,12},{12,14},{14,0},{1,3},{3,5},... | collective-permute-start | bytes 1277960 | tf_op jit(solution)/shard_map/ppermute | solution.py:548
  4.4 0.0 collective-permute-start.3
  4.4 2.9 %collective-permute-start.1 = (f32[4,104,128]{2,1,0:T(8,128)S(1)}, f32[4,104,128]{2,1,0:T(8,128)S(1)}, u32[]{:S(2)}, u32[]{:S(2)}) collective-permute-start(f32[4,104,128]{2,1,0:T(8,128)S(1)} %get-tuple-element.48.a0), channel_id=1, source_target_pairs={{0,113},{1,0},{16,1},{17,16},{32,17},{33,32},{48,33},{49,48},{64,4... | collective-permute-start | bytes 638984 | tf_op jit(solution)/shard_map/ppermute | solution.py:548
  7.3 0.1 collective-permute-start
  7.4 2.1 %collective-permute-done.2.hzm = f32[8,104,128]{2,1,0:T(8,128)S(1)} collective-permute-done((f32[8,104,128]{2,1,0:T(8,128)S(1)}, f32[8,104,128]{2,1,0:T(8,128)S(1)}, u32[]{:S(2)}, u32[]{:S(2)}) %collective-permute-start.2) | collective-permute-done | bytes 426016 | tf_op jit(solution)/shard_map/ppermute | solution.py:548
  9.5 2.8 %collective-permute-done.3.hzp = f32[8,104,128]{2,1,0:T(8,128)S(1)} collective-permute-done((f32[8,104,128]{2,1,0:T(8,128)S(1)}, f32[8,104,128]{2,1,0:T(8,128)S(1)}, u32[]{:S(2)}, u32[]{:S(2)}) %collective-permute-start.3) | collective-permute-done | bytes 426016 | tf_op jit(solution)/shard_map/ppermute | solution.py:548
  12.3 3.0 %collective-permute-start.4 = (f32[2,96,128]{2,1,0:T(8,128)S(1)}, f32[2,96,128]{2,1,0:T(8,128)S(1)}, u32[]{:S(2)}, u32[]{:S(2)}) collective-permute-start(f32[2,96,128]{2,1,0:T(8,128)S(1)} %pad_maximum_fusion), channel_id=1, source_target_pairs={{0,1},{1,16},{16,17},{17,32},{32,33},{33,48},{48,49},{49,64},{64,6... | collective-permute-start | bytes 294920 | tf_op jit(solution)/shard_map/ppermute | solution.py:548
  15.3 1.0 %collective-permute-start.5 = (f32[2,96,128]{2,1,0:T(8,128)S(1)}, f32[2,96,128]{2,1,0:T(8,128)S(1)}, u32[]{:S(2)}, u32[]{:S(2)}) collective-permute-start(f32[2,96,128]{2,1,0:T(8,128)S(1)} %pad_maximum_fusion.1), channel_id=1, source_target_pairs={{0,113},{1,0},{16,1},{17,16},{32,17},{33,32},{48,33},{49,48},{64,4... | collective-permute-start | bytes 294920 | tf_op jit(solution)/shard_map/ppermute | solution.py:548
  16.3 0.6 shard_map.123
  16.9 2.7 %shard_map.124 = (f32[64,96,128]{2,1,0:T(8,128)S(1)}, f32[64,8,128]{2,1,0:T(8,128)S(1)}, f32[64,96,128]{2,1,0:T(8,128)S(1)}) custom-call(f32[4,104,128]{2,1,0:T(8,128)S(1)} %get-tuple-element.48.a0, f32[4,96,128]{2,1,0:T(8,128)S(1)} %get-tuple-element.49.a1, f32[4,96,128]{2,1,0:T(8,128)S(1)} %get-tuple-element.50.a2, ...), custom_call_target="tpu_custom_call" | custom-call | tf_op jit(solution)/shard_map/pallas_call | solution.py:541
  19.6 2.0 %shard_map.125.x1_in = f32[64,96,128]{2,1,0:T(8,128)S(1)} custom-call(f32[64,96,128]{2,1,0:T(8,128)S(1)} %get-tuple-element.66.x0.x0_in, f32[64,8,128]{2,1,0:T(8,128)S(1)} %get-tuple-element.67.lw.lw_in, f32[64,96,128]{2,1,0:T(8,128)S(1)} %get-tuple-element.68.x1_in, bf16[192,864]{1,0:T(8,128)(2,1)S(1)} %get-tuple-element.65.mmat, ...), custom_call_target="tpu_custom_call", output_to_operand_aliasing={{}: (2, {})} | custom-call | tf_op jit(solution)/shard_map/pallas_call | solution.py:541
  21.6 0.0 collective-permute-done.1.tp1
  21.6 0.0 collective-permute-done.tm1
  21.7 0.0 copy-start
  21.7 6.7 %shard_map.126 = (f32[64,96,128]{2,1,0:T(8,128)S(1)}, f32[64,8,128]{2,1,0:T(8,128)S(1)}, f32[64,96,128]{2,1,0:T(8,128)S(1)}, f32[20,8,128]{2,1,0:T(8,128)S(1)}, ...) custom-call(f32[4,104,128]{2,1,0:T(8,128)S(1)} %get-tuple-element.48, ...), custom_call_target="tpu_custom_call", output_to_operand_aliasing={{0}: (15, {}), {1}: (16, {}), {2}: (17, {})} | custom-call | tf_op jit(solution)/shard_map/pallas_call | solution.py:541
  28.4 2.3 %collective-permute-start.6 = (f32[20,8,128]{2,1,0:T(8,128)S(1)}, f32[20,8,128]{2,1,0:T(8,128)S(1)}, u32[]{:S(2)}, u32[]{:S(2)}) collective-permute-start(f32[20,8,128]{2,1,0:T(8,128)S(1)} %get-tuple-element.69.up), channel_id=1, source_target_pairs={{0,1},{1,16},{16,17},{17,32},{32,33},{33,48},{48,49},{49,64},{64,6... | collective-permute-start | bytes 245768 | tf_op jit(solution)/shard_map/ppermute | solution.py:548
  30.8 1.6 %collective-permute-start.7 = (f32[20,8,128]{2,1,0:T(8,128)S(1)}, f32[20,8,128]{2,1,0:T(8,128)S(1)}, u32[]{:S(2)}, u32[]{:S(2)}) collective-permute-start(f32[20,8,128]{2,1,0:T(8,128)S(1)} %get-tuple-element.70.down), channel_id=1, source_target_pairs={{0,113},{1,0},{16,1},{17,16},{32,17},{33,32},{48,33},{49,48},{64,4... | collective-permute-start | bytes 245768 | tf_op jit(solution)/shard_map/ppermute | solution.py:548
  32.4 1.4 %collective-permute-start.12 = (f32[4,96,128]{2,1,0:T(8,128)S(1)}, f32[4,96,128]{2,1,0:T(8,128)S(1)}, u32[]{:S(2)}, u32[]{:S(2)}) collective-permute-start(f32[4,96,128]{2,1,0:T(8,128)S(1)} %get-tuple-element.77), channel_id=1, source_target_pairs={{0,1},{1,16},{16,17},{17,32},{32,33},{33,48},{48,49},{49,64},{64,6... | collective-permute-start | bytes 589832 | tf_op jit(solution)/shard_map/ppermute | solution.py:548
  33.8 2.5 %collective-permute-start.13 = (f32[4,96,128]{2,1,0:T(8,128)S(1)}, f32[4,96,128]{2,1,0:T(8,128)S(1)}, u32[]{:S(2)}, u32[]{:S(2)}) collective-permute-start(f32[4,96,128]{2,1,0:T(8,128)S(1)} %get-tuple-element.78), channel_id=1, source_target_pairs={{0,113},{1,0},{16,1},{17,16},{32,17},{33,32},{48,33},{49,48},{64,4... | collective-permute-start | bytes 589832 | tf_op jit(solution)/shard_map/ppermute | solution.py:548
  36.3 0.0 collective-permute-done.6.tcm
  36.3 0.1 collective-permute-done.7.tcp
  36.4 6.6 %collective-permute-start.11 = (f32[40,8,128]{2,1,0:T(8,128)S(1)}, f32[40,8,128]{2,1,0:T(8,128)S(1)}, u32[]{:S(2)}, u32[]{:S(2)}) collective-permute-start(f32[40,8,128]{2,1,0:T(8,128)S(1)} %get-tuple-element.72), channel_id=1, source_target_pairs={{0,14},{2,0},{4,2},{6,4},{8,6},{10,8},{12,10},{14,12},{1,15},{3,1}... | collective-permute-start | bytes 491528 | tf_op jit(solution)/shard_map/ppermute | solution.py:548
  43.0 1.6 %collective-permute-start.10 = (f32[40,8,128]{2,1,0:T(8,128)S(1)}, f32[40,8,128]{2,1,0:T(8,128)S(1)}, u32[]{:S(2)}, u32[]{:S(2)}) collective-permute-start(f32[40,8,128]{2,1,0:T(8,128)S(1)} %get-tuple-element.72), channel_id=1, source_target_pairs={{0,2},{2,4},{4,6},{6,8},{8,10},{10,12},{12,14},{14,0},{1,3},{3,5},... | collective-permute-start | bytes 491528 | tf_op jit(solution)/shard_map/ppermute | solution.py:548
  44.5 0.1 collective-permute-start.9
  44.6 2.8 %collective-permute-done.9.e2p = f32[4,8,128]{2,1,0:T(8,128)S(1)} collective-permute-done((f32[4,8,128]{2,1,0:T(8,128)S(1)}, f32[4,8,128]{2,1,0:T(8,128)S(1)}, u32[]{:S(2)}, u32[]{:S(2)}) %collective-permute-start.9) | collective-permute-done | bytes 16416 | tf_op jit(solution)/shard_map/ppermute | solution.py:548
  47.4 3.2 %collective-permute-start.8 = (f32[4,8,128]{2,1,0:T(8,128)S(1)}, f32[4,8,128]{2,1,0:T(8,128)S(1)}, u32[]{:S(2)}, u32[]{:S(2)}) collective-permute-start(f32[4,8,128]{2,1,0:T(8,128)S(1)} %slice.34), channel_id=1, source_target_pairs={{0,16},{1,17},{16,32},{17,33},{32,48},{33,49},{48,64},{49,65},{64,... | collective-permute-start | bytes 49160 | tf_op jit(solution)/shard_map/ppermute | solution.py:548
  50.6 1.9 %shard_map.128 = (bf16[2304,256]{1,0:T(8,128)(2,1)S(1)}, bf16[256,256]{1,0:T(8,128)(2,1)S(1)}, f32[96,128]{1,0:T(8,128)S(1)}) custom-call(f32[128,128]{1,0:T(8,128)} %cs_far.1, f32[9,128,128]{2,1,0:T(8,128)} %coarse_far.1, f32[96,128]{1,0:T(8,128)} %bitcast.8), custom_call_target="tpu_custom_call" | custom-call | tf_op jit(solution)/shard_map/pallas_call | solution.py:541
  52.5 0.0 collective-permute-done.11.zcp
  52.5 0.0 collective-permute-done.10.zcm
  52.5 0.1 broadcast_in_dim.2.coarse_ref
  52.6 4.0 %shard_map.129.lifted = f32[3,96,128]{2,1,0:T(8,128)S(1)} custom-call(f32[48,8,128]{2,1,0:T(8,128)S(1)} %get-tuple-element.71.whole, f32[4,8,128]{2,1,0:T(8,128)S(1)} %collective-permute-done.8.e2m, f32[4,8,128]{2,1,0:T(8,128)S(1)} %collective-permute-done.9.e2p, f32[40,8,128]{2,1,0:T(8,128)S(1)} %collective-permute-done.10.zcm, ...), custom_call_target="tpu_custom_call" | custom-call | tf_op jit(solution)/shard_map/pallas_call | solution.py:541
  56.6 0.0 collective-permute-done.13.xp
  56.6 3.0 %shard_map.130 = (f32[64,96,128]{2,1,0:T(8,128)S(1)}, f32[64,96,128]{2,1,0:T(8,128)S(1)}, f32[4,96,128]{2,1,0:T(8,128)S(1)}, f32[4,96,128]{2,1,0:T(8,128)S(1)}) custom-call(f32[3,96,128]{2,1,0:T(8,128)S(1)} %shard_map.129.lifted, s32[1,128]{1,0:T(1,128)S(1)} %get-tuple-element.56.home.lift_ref, s32[4,128]{1,0:T(4,128)S(1)} %get-tuple-element.62.plane_ref, ...), custom_call_target="tpu_custom_call" | custom-call | tf_op jit(solution)/shard_map/pallas_call | solution.py:541
  59.7 0.1 collective-permute-start.18
  59.8 3.0 %collective-permute-start.16 = (f32[4,96,128]{2,1,0:T(8,128)S(1)}, f32[4,96,128]{2,1,0:T(8,128)S(1)}, u32[]{:S(2)}, u32[]{:S(2)}) collective-permute-start(f32[4,96,128]{2,1,0:T(8,128)S(1)} %get-tuple-element.84.last), channel_id=1, source_target_pairs={{0,1},{1,16},{16,17},{17,32},{32,33},{33,48},{48,49},{49,64},{64,6... | collective-permute-start | bytes 589832 | tf_op jit(solution)/shard_map/ppermute | solution.py:548
  62.7 1.4 %shard_map.131 = (f32[64,96,128]{2,1,0:T(8,128)S(1)}, f32[4,96,128]{2,1,0:T(8,128)S(1)}, f32[4,96,128]{2,1,0:T(8,128)S(1)}, f32[8,96,128]{2,1,0:T(8,128)S(1)}, f32[8,96,128]{2,1,0:T(8,128)S(1)}) custom-call(f32[64,96,128]{2,1,0:T(8,128)S(1)} %get-tuple-element.81.field, ...), custom_call_target="tpu_custom_call", output_to_operand_aliasing={{0}: (1, {})} | custom-call | tf_op jit(solution)/shard_map/pallas_call | solution.py:541
  64.1 0.5 collective-permute-start.17
  64.6 3.4 %collective-permute-start.19 = (f32[4,96,128]{2,1,0:T(8,128)S(1)}, f32[4,96,128]{2,1,0:T(8,128)S(1)}, u32[]{:S(2)}, u32[]{:S(2)}) collective-permute-start(f32[4,96,128]{2,1,0:T(8,128)S(1)} %get-tuple-element.91), channel_id=1, source_target_pairs={{0,113},{1,0},{16,1},{17,16},{32,17},{33,32},{48,33},{49,48},{64,4... | collective-permute-start | bytes 589832 | tf_op jit(solution)/shard_map/ppermute | solution.py:548
  68.0 3.0 %collective-permute-start.14 = (f32[8,96,128]{2,1,0:T(8,128)S(1)}, f32[8,96,128]{2,1,0:T(8,128)S(1)}, u32[]{:S(2)}, u32[]{:S(2)}) collective-permute-start(f32[8,96,128]{2,1,0:T(8,128)S(1)} %get-tuple-element.86), channel_id=1, source_target_pairs={{0,2},{2,4},{4,6},{6,8},{8,10},{10,12},{12,14},{14,0},{1,3},{3,5},... | collective-permute-start | bytes 1179656 | tf_op jit(solution)/shard_map/ppermute | solution.py:548
  71.1 4.8 %collective-permute-done.18.tp1 = f32[4,96,128]{2,1,0:T(8,128)S(1)} collective-permute-done((f32[4,96,128]{2,1,0:T(8,128)S(1)}, f32[4,96,128]{2,1,0:T(8,128)S(1)}, u32[]{:S(2)}, u32[]{:S(2)}) %collective-permute-start.18) | collective-permute-done | bytes 196640 | tf_op jit(solution)/shard_map/ppermute | solution.py:548
  75.9 1.7 %collective-permute-start.15 = (f32[8,96,128]{2,1,0:T(8,128)S(1)}, f32[8,96,128]{2,1,0:T(8,128)S(1)}, u32[]{:S(2)}, u32[]{:S(2)}) collective-permute-start(f32[8,96,128]{2,1,0:T(8,128)S(1)} %get-tuple-element.87), channel_id=1, source_target_pairs={{0,14},{2,0},{4,2},{6,4},{8,6},{10,8},{12,10},{14,12},{1,15},{3,1}... | collective-permute-start | bytes 1179656 | tf_op jit(solution)/shard_map/ppermute | solution.py:548
  77.7 0.0 collective-permute-done.16.tm1
  77.7 1.7 %collective-permute-start.20 = (f32[2,96,128]{2,1,0:T(8,128)S(1)}, f32[2,96,128]{2,1,0:T(8,128)S(1)}, u32[]{:S(2)}, u32[]{:S(2)}) collective-permute-start(f32[2,96,128]{2,1,0:T(8,128)S(1)} %pad_maximum_fusion.2), channel_id=1, source_target_pairs={{0,2},{2,4},{4,6},{6,8},{8,10},{10,12},{12,14},{14,0},{1,3},{3,5},... | collective-permute-start | bytes 294920 | tf_op jit(solution)/shard_map/ppermute | solution.py:548
  79.4 0.0 collective-permute-start.21
  79.4 5.3 %collective-permute-done.15.hzp = f32[8,96,128]{2,1,0:T(8,128)S(1)} collective-permute-done((f32[8,96,128]{2,1,0:T(8,128)S(1)}, f32[8,96,128]{2,1,0:T(8,128)S(1)}, u32[]{:S(2)}, u32[]{:S(2)}) %collective-permute-start.15) | collective-permute-done | bytes 393248 | tf_op jit(solution)/shard_map/ppermute | solution.py:548
  84.8 4.0 %shard_map.132 = (f32[64,96,128]{2,1,0:T(8,128)S(1)}, f32[64,96,128]{2,1,0:T(8,128)S(1)}) custom-call(f32[64,96,128]{2,1,0:T(8,128)S(1)} %get-tuple-element.85.wide_in, f32[8,96,128]{2,1,0:T(8,128)S(1)} %collective-permute-done.14.hzm, f32[8,96,128]{2,1,0:T(8,128)S(1)} %collective-permute-done.15.hzp, ...), custom_call_target="tpu_custom_call", output_to_operand_aliasing={{0}: (0, {})} | custom-call | tf_op jit(solution)/shard_map/pallas_call | solution.py:541
  88.8 5.2 %shard_map.133 = (f32[64,96,128]{2,1,0:T(8,128)S(1)}, f32[64,96,128]{2,1,0:T(8,128)S(1)}, f32[96,16,128]{2,1,0:T(8,128)}, f32[96,16,128]{2,1,0:T(8,128)}) custom-call(f32[64,96,128]{2,1,0:T(8,128)S(1)} %get-tuple-element.88.wide_in, f32[64,96,128]{2,1,0:T(8,128)S(1)} %get-tuple-element.89.x4_in, ...), custom_call_target="tpu_custom_call", output_to_operand_aliasing={{0}: (0, {}), {1}: (1, {})} | custom-call | tf_op jit(solution)/shard_map/pallas_call | solution.py:541
  (21 shorter events, 0.1 us)
Async XLA Ops:
  2.2 7.3 %collective-permute-start.2 = (f32[8,104,128]{2,1,0:T(8,128)S(1)}, f32[8,104,128]{2,1,0:T(8,128)S(1)}, u32[]{:S(2)}, u32[]{:S(2)}) collective-permute-start(f32[8,104,128]{2,1,0:T(8,128)S(1)} %get-tuple-element.52), channel_id=1, source_target_pairs={{0,2},{2,4},{4,6},{6,8},{8,10},{10,12},{12,14},{14,0},{1,3},{3,5},... | collective-permute-start | bytes 1277960 | tf_op jit(solution)/shard_map/ppermute | solution.py:548
  4.4 7.8 %collective-permute-start.3 = (f32[8,104,128]{2,1,0:T(8,128)S(1)}, f32[8,104,128]{2,1,0:T(8,128)S(1)}, u32[]{:S(2)}, u32[]{:S(2)}) collective-permute-start(f32[8,104,128]{2,1,0:T(8,128)S(1)} %get-tuple-element.53), channel_id=1, source_target_pairs={{0,14},{2,0},{4,2},{6,4},{8,6},{10,8},{12,10},{14,12},{1,15},{3,1}... | collective-permute-start | bytes 1277960 | tf_op jit(solution)/shard_map/ppermute | solution.py:548
  4.4 17.3 %collective-permute-start.1 = (f32[4,104,128]{2,1,0:T(8,128)S(1)}, f32[4,104,128]{2,1,0:T(8,128)S(1)}, u32[]{:S(2)}, u32[]{:S(2)}) collective-permute-start(f32[4,104,128]{2,1,0:T(8,128)S(1)} %get-tuple-element.48.a0), channel_id=1, source_target_pairs={{0,113},{1,0},{16,1},{17,16},{32,17},{33,32},{48,33},{49,48},{64,4... | collective-permute-start | bytes 638984 | tf_op jit(solution)/shard_map/ppermute | solution.py:548
  7.3 14.4 %collective-permute-start = (f32[4,104,128]{2,1,0:T(8,128)S(1)}, f32[4,104,128]{2,1,0:T(8,128)S(1)}, u32[]{:S(2)}, u32[]{:S(2)}) collective-permute-start(f32[4,104,128]{2,1,0:T(8,128)S(1)} %get-tuple-element.51.a3), channel_id=1, source_target_pairs={{0,1},{1,16},{16,17},{17,32},{32,33},{33,48},{48,49},{49,64},{64,6... | collective-permute-start | bytes 638984 | tf_op jit(solution)/shard_map/ppermute | solution.py:548
  12.3 9.4 %collective-permute-start.4 = (f32[2,96,128]{2,1,0:T(8,128)S(1)}, f32[2,96,128]{2,1,0:T(8,128)S(1)}, u32[]{:S(2)}, u32[]{:S(2)}) collective-permute-start(f32[2,96,128]{2,1,0:T(8,128)S(1)} %pad_maximum_fusion), channel_id=1, source_target_pairs={{0,1},{1,16},{16,17},{17,32},{32,33},{33,48},{48,49},{49,64},{64,6... | collective-permute-start | bytes 294920 | tf_op jit(solution)/shard_map/ppermute | solution.py:548
  15.3 6.4 %collective-permute-start.5 = (f32[2,96,128]{2,1,0:T(8,128)S(1)}, f32[2,96,128]{2,1,0:T(8,128)S(1)}, u32[]{:S(2)}, u32[]{:S(2)}) collective-permute-start(f32[2,96,128]{2,1,0:T(8,128)S(1)} %pad_maximum_fusion.1), channel_id=1, source_target_pairs={{0,113},{1,0},{16,1},{17,16},{32,17},{33,32},{48,33},{49,48},{64,4... | collective-permute-start | bytes 294920 | tf_op jit(solution)/shard_map/ppermute | solution.py:548
  21.7 30.8 %copy-start = (s32[4,8]{1,0:T(4,128)S(1)}, s32[4,8]{1,0:T(4,128)}, u32[]{:S(2)}) copy-start(s32[4,8]{1,0:T(4,128)} %param.21) | copy-start | bytes 388
  28.4 7.8 %collective-permute-start.6 = (f32[20,8,128]{2,1,0:T(8,128)S(1)}, f32[20,8,128]{2,1,0:T(8,128)S(1)}, u32[]{:S(2)}, u32[]{:S(2)}) collective-permute-start(f32[20,8,128]{2,1,0:T(8,128)S(1)} %get-tuple-element.69.up), channel_id=1, source_target_pairs={{0,1},{1,16},{16,17},{17,32},{32,33},{33,48},{48,49},{49,64},{64,6... | collective-permute-start | bytes 245768 | tf_op jit(solution)/shard_map/ppermute | solution.py:548
  30.8 5.6 %collective-permute-start.7 = (f32[20,8,128]{2,1,0:T(8,128)S(1)}, f32[20,8,128]{2,1,0:T(8,128)S(1)}, u32[]{:S(2)}, u32[]{:S(2)}) collective-permute-start(f32[20,8,128]{2,1,0:T(8,128)S(1)} %get-tuple-element.70.down), channel_id=1, source_target_pairs={{0,113},{1,0},{16,1},{17,16},{32,17},{33,32},{48,33},{49,48},{64,4... | collective-permute-start | bytes 245768 | tf_op jit(solution)/shard_map/ppermute | solution.py:548
  32.4 24.2 %collective-permute-start.12 = (f32[4,96,128]{2,1,0:T(8,128)S(1)}, f32[4,96,128]{2,1,0:T(8,128)S(1)}, u32[]{:S(2)}, u32[]{:S(2)}) collective-permute-start(f32[4,96,128]{2,1,0:T(8,128)S(1)} %get-tuple-element.77), channel_id=1, source_target_pairs={{0,1},{1,16},{16,17},{17,32},{32,33},{33,48},{48,49},{49,64},{64,6... | collective-permute-start | bytes 589832 | tf_op jit(solution)/shard_map/ppermute | solution.py:548
  33.8 22.9 %collective-permute-start.13 = (f32[4,96,128]{2,1,0:T(8,128)S(1)}, f32[4,96,128]{2,1,0:T(8,128)S(1)}, u32[]{:S(2)}, u32[]{:S(2)}) collective-permute-start(f32[4,96,128]{2,1,0:T(8,128)S(1)} %get-tuple-element.78), channel_id=1, source_target_pairs={{0,113},{1,0},{16,1},{17,16},{32,17},{33,32},{48,33},{49,48},{64,4... | collective-permute-start | bytes 589832 | tf_op jit(solution)/shard_map/ppermute | solution.py:548
  36.4 16.1 %collective-permute-start.11 = (f32[40,8,128]{2,1,0:T(8,128)S(1)}, f32[40,8,128]{2,1,0:T(8,128)S(1)}, u32[]{:S(2)}, u32[]{:S(2)}) collective-permute-start(f32[40,8,128]{2,1,0:T(8,128)S(1)} %get-tuple-element.72), channel_id=1, source_target_pairs={{0,14},{2,0},{4,2},{6,4},{8,6},{10,8},{12,10},{14,12},{1,15},{3,1}... | collective-permute-start | bytes 491528 | tf_op jit(solution)/shard_map/ppermute | solution.py:548
  43.0 9.5 %collective-permute-start.10 = (f32[40,8,128]{2,1,0:T(8,128)S(1)}, f32[40,8,128]{2,1,0:T(8,128)S(1)}, u32[]{:S(2)}, u32[]{:S(2)}) collective-permute-start(f32[40,8,128]{2,1,0:T(8,128)S(1)} %get-tuple-element.72), channel_id=1, source_target_pairs={{0,2},{2,4},{4,6},{6,8},{8,10},{10,12},{12,14},{14,0},{1,3},{3,5},... | collective-permute-start | bytes 491528 | tf_op jit(solution)/shard_map/ppermute | solution.py:548
  44.5 2.9 %collective-permute-start.9 = (f32[4,8,128]{2,1,0:T(8,128)S(1)}, f32[4,8,128]{2,1,0:T(8,128)S(1)}, u32[]{:S(2)}, u32[]{:S(2)}) collective-permute-start(f32[4,8,128]{2,1,0:T(8,128)S(1)} %slice.35), channel_id=1, source_target_pairs={{0,112},{1,113},{16,0},{17,1},{32,16},{33,17},{48,32},{49,33},{64,... | collective-permute-start | bytes 49160 | tf_op jit(solution)/shard_map/ppermute | solution.py:548
  47.4 5.1 %collective-permute-start.8 = (f32[4,8,128]{2,1,0:T(8,128)S(1)}, f32[4,8,128]{2,1,0:T(8,128)S(1)}, u32[]{:S(2)}, u32[]{:S(2)}) collective-permute-start(f32[4,8,128]{2,1,0:T(8,128)S(1)} %slice.34), channel_id=1, source_target_pairs={{0,16},{1,17},{16,32},{17,33},{32,48},{33,49},{48,64},{49,65},{64,... | collective-permute-start | bytes 49160 | tf_op jit(solution)/shard_map/ppermute | solution.py:548
  59.7 16.2 %collective-permute-start.18 = (f32[4,96,128]{2,1,0:T(8,128)S(1)}, f32[4,96,128]{2,1,0:T(8,128)S(1)}, u32[]{:S(2)}, u32[]{:S(2)}) collective-permute-start(f32[4,96,128]{2,1,0:T(8,128)S(1)} %get-tuple-element.83.first), channel_id=1, source_target_pairs={{0,113},{1,0},{16,1},{17,16},{32,17},{33,32},{48,33},{49,48},{64,4... | collective-permute-start | bytes 589832 | tf_op jit(solution)/shard_map/ppermute | solution.py:548
  59.8 17.9 %collective-permute-start.16 = (f32[4,96,128]{2,1,0:T(8,128)S(1)}, f32[4,96,128]{2,1,0:T(8,128)S(1)}, u32[]{:S(2)}, u32[]{:S(2)}) collective-permute-start(f32[4,96,128]{2,1,0:T(8,128)S(1)} %get-tuple-element.84.last), channel_id=1, source_target_pairs={{0,1},{1,16},{16,17},{17,32},{32,33},{33,48},{48,49},{49,64},{64,6... | collective-permute-start | bytes 589832 | tf_op jit(solution)/shard_map/ppermute | solution.py:548
  64.1 24.7 %collective-permute-start.17 = (f32[4,96,128]{2,1,0:T(8,128)S(1)}, f32[4,96,128]{2,1,0:T(8,128)S(1)}, u32[]{:S(2)}, u32[]{:S(2)}) collective-permute-start(f32[4,96,128]{2,1,0:T(8,128)S(1)} %get-tuple-element.90), channel_id=1, source_target_pairs={{0,1},{1,16},{16,17},{17,32},{32,33},{33,48},{48,49},{49,64},{64,6... | collective-permute-start | bytes 589832 | tf_op jit(solution)/shard_map/ppermute | solution.py:548
  64.6 24.1 %collective-permute-start.19 = (f32[4,96,128]{2,1,0:T(8,128)S(1)}, f32[4,96,128]{2,1,0:T(8,128)S(1)}, u32[]{:S(2)}, u32[]{:S(2)}) collective-permute-start(f32[4,96,128]{2,1,0:T(8,128)S(1)} %get-tuple-element.91), channel_id=1, source_target_pairs={{0,113},{1,0},{16,1},{17,16},{32,17},{33,32},{48,33},{49,48},{64,4... | collective-permute-start | bytes 589832 | tf_op jit(solution)/shard_map/ppermute | solution.py:548
  68.0 11.3 %collective-permute-start.14 = (f32[8,96,128]{2,1,0:T(8,128)S(1)}, f32[8,96,128]{2,1,0:T(8,128)S(1)}, u32[]{:S(2)}, u32[]{:S(2)}) collective-permute-start(f32[8,96,128]{2,1,0:T(8,128)S(1)} %get-tuple-element.86), channel_id=1, source_target_pairs={{0,2},{2,4},{4,6},{6,8},{8,10},{10,12},{12,14},{14,0},{1,3},{3,5},... | collective-permute-start | bytes 1179656 | tf_op jit(solution)/shard_map/ppermute | solution.py:548
  75.9 8.8 %collective-permute-start.15 = (f32[8,96,128]{2,1,0:T(8,128)S(1)}, f32[8,96,128]{2,1,0:T(8,128)S(1)}, u32[]{:S(2)}, u32[]{:S(2)}) collective-permute-start(f32[8,96,128]{2,1,0:T(8,128)S(1)} %get-tuple-element.87), channel_id=1, source_target_pairs={{0,14},{2,0},{4,2},{6,4},{8,6},{10,8},{12,10},{14,12},{1,15},{3,1}... | collective-permute-start | bytes 1179656 | tf_op jit(solution)/shard_map/ppermute | solution.py:548
  77.7 11.1 %collective-permute-start.20 = (f32[2,96,128]{2,1,0:T(8,128)S(1)}, f32[2,96,128]{2,1,0:T(8,128)S(1)}, u32[]{:S(2)}, u32[]{:S(2)}) collective-permute-start(f32[2,96,128]{2,1,0:T(8,128)S(1)} %pad_maximum_fusion.2), channel_id=1, source_target_pairs={{0,2},{2,4},{4,6},{6,8},{8,10},{10,12},{12,14},{14,0},{1,3},{3,5},... | collective-permute-start | bytes 294920 | tf_op jit(solution)/shard_map/ppermute | solution.py:548
  79.4 9.4 %collective-permute-start.21 = (f32[2,96,128]{2,1,0:T(8,128)S(1)}, f32[2,96,128]{2,1,0:T(8,128)S(1)}, u32[]{:S(2)}, u32[]{:S(2)}) collective-permute-start(f32[2,96,128]{2,1,0:T(8,128)S(1)} %pad_maximum_fusion.3), channel_id=1, source_target_pairs={{0,14},{2,0},{4,2},{6,4},{8,6},{10,8},{12,10},{14,12},{1,15},{3,1}... | collective-permute-start | bytes 294920 | tf_op jit(solution)/shard_map/ppermute | solution.py:548
